TPU v7x, 128 devices: a whole 4x4x4 slice. The times are simulated.
128 devices in a mesh: row: 16 (over z_hi, y, core), col: 8 (over z_lo, x).
Axes of the slice: x: 4, y: 4, z: 4 (z_hi: 2, z_lo: 2; z = z_hi * 2 + z_lo), core: 2. Of those that a mesh axis runs over, the one named last changes fastest.
Arguments:
- multispectral: bfloat16 [2, 32768, 4096], P(None, 'row', 'col'), may hold values from -6 to 6
- hyperspectral: bfloat16 [96, 8192, 1024], P(None, 'row', 'col'), may hold values from -6 to 6
- row_start: float32 [32768, 128], P(('row', 'col')), may hold values from -6 to 6
- col_factor: bfloat16 [4096, 128], P('col', 'row'), may hold values from -0.09375 to 0.09375
- band_factor: float32 [96, 128], replicated, may hold values from -2 to 2
- response: float32 [2, 96], replicated, may hold values from 0.2 to 1
- blur_taps: float32 [9], replicated, may hold values from 0.2 to 1
- offsets: int32 [9], replicated, may hold values from -8 to 8, as said below
Outputs:
- row_factor: float32 [32768, 128], P(('row', 'col'))
- residual: float32 [32768, 128], P(('row', 'col'))
Inputs may be any that keep to these rules, and one draw needn't show every extreme that they name: 9 distinct offsets; -8 and 8 are always among them.
All inputs are finite; a program needn't handle non-finite values.
Results may differ from a plain program's by a relative error of at most 0.0023.
Values may be sent and summed in bfloat16 or wider, within the bound.
A program may use at most 128 MiB of HBM per device.

v0:
```python
import functools

import jax
import jax.numpy as jnp
from jax import lax
from jax.experimental import pallas as pl
from jax.experimental.pallas import tpu as pltpu
from jax.sharding import PartitionSpec as P

MESH = pl.DeviceIdType.MESH

DEC = 4
W = 8
ITERS = 4


RIDGE_TERM = 0.1
FULL_PRECISION = lax.Precision.HIGHEST


def extended(cells, sides, width):
    for axis, dim in sides:
        names = axis if isinstance(axis, tuple) else (axis,)
        count = 1
        for name in names:
            count *= lax.axis_size(name)
        head = lax.slice_in_dim(cells, 0, width, axis=dim)
        tail = lax.slice_in_dim(cells, cells.shape[dim] - width, cells.shape[dim], axis=dim)
        cells = jnp.concatenate(
            [
                lax.ppermute(tail, axis, [(i, (i + 1) % count) for i in range(count)]),
                cells,
                lax.ppermute(head, axis, [((i + 1) % count, i) for i in range(count)]),
            ],
            axis=dim,
        )
    return cells


def tap_places(offsets):
    reach = offsets + W
    return reach // DEC, reach % DEC


def blur_down(wide, weights, offsets, rows_out):
    shifts, phases = tap_places(offsets)
    quads = wide.reshape(wide.shape[0] // DEC, DEC, wide.shape[1])
    total = jnp.zeros((rows_out, wide.shape[1]), jnp.float32)
    for number in range(weights.shape[0]):
        piece = lax.dynamic_slice(
            quads, (shifts[number], phases[number], 0), (rows_out, 1, wide.shape[1])
        )[:, 0, :]
        total = total + weights[number] * piece.astype(jnp.float32)
    return total


def blur_up(coarse_wide, weights, offsets, margin):
    shifts, phases = tap_places(offsets)
    rows = coarse_wide.shape[0] - 2 * margin
    columns = coarse_wide.shape[1]
    parts = [jnp.zeros((rows, columns), jnp.float32) for _ in range(DEC)]
    for number in range(weights.shape[0]):
        piece = lax.dynamic_slice_in_dim(coarse_wide, margin + 2 - shifts[number], rows, 0)
        for phase in range(DEC):
            scale = jnp.where(phases[number] == phase, weights[number], jnp.float32(0.0))
            parts[phase] = parts[phase] + scale * piece
    return jnp.stack(parts, axis=1).reshape(rows * DEC, columns)


def total_kernel(rows, cols, part_ref, out_ref, col_held, row_held, sends, receipts):
    here_row = lax.axis_index("row")
    here_col = lax.axis_index("col")
    col_peers = [(here_row, lax.rem(here_col + shift, cols)) for shift in range(1, cols)]
    row_peers = [(lax.rem(here_row + shift, rows), here_col) for shift in range(1, rows)]
    barrier = pltpu.get_barrier_semaphore()
    for peer in col_peers + row_peers:
        pl.semaphore_signal(barrier, inc=1, device_id=peer, device_id_type=MESH)
    pl.semaphore_wait(barrier, len(col_peers) + len(row_peers))
    copies = []
    for number, peer in enumerate(col_peers):
        copy = pltpu.make_async_remote_copy(
            src_ref=part_ref,
            dst_ref=col_held.at[here_col],
            send_sem=sends.at[number],
            recv_sem=receipts.at[number],
            device_id=peer,
            device_id_type=MESH,
        )
        copy.start()
        copies.append(copy)
    col_held[here_col] = part_ref[...]
    for copy in copies:
        copy.wait()
    col_total = col_held[0]
    for source in range(1, cols):
        col_total = col_total + col_held[source]
    row_held[here_row] = col_total
    copies = []
    for number, peer in enumerate(row_peers):
        copy = pltpu.make_async_remote_copy(
            src_ref=row_held.at[here_row],
            dst_ref=row_held.at[here_row],
            send_sem=sends.at[cols + number],
            recv_sem=receipts.at[cols + number],
            device_id=peer,
            device_id_type=MESH,
        )
        copy.start()
        copies.append(copy)
    for copy in copies:
        copy.wait()
    total = row_held[0]
    for source in range(1, rows):
        total = total + row_held[source]
    out_ref[...] = total


def grid_totals(parts):
    rows = lax.axis_size("row")
    cols = lax.axis_size("col")
    lanes = jnp.pad(jnp.stack(parts), (0, 128 - len(parts)))
    tile = jnp.broadcast_to(lanes[None, :], (8, 128))
    summed = pl.pallas_call(
        functools.partial(total_kernel, rows, cols),
        out_shape=jax.ShapeDtypeStruct((8, 128), jnp.float32),
        in_specs=[pl.BlockSpec(memory_space=pltpu.VMEM)],
        out_specs=pl.BlockSpec(memory_space=pltpu.VMEM),
        scratch_shapes=[
            pltpu.VMEM((cols, 8, 128), jnp.float32),
            pltpu.VMEM((rows, 8, 128), jnp.float32),
            pltpu.SemaphoreType.DMA((rows + cols,)),
            pltpu.SemaphoreType.DMA((rows + cols,)),
        ],
        compiler_params=pltpu.CompilerParams(collective_id=0, has_side_effects=True),
    )(tile)
    return [summed[0, number] for number in range(len(parts))]


def body(
    multispectral, hyperspectral, row_start, col_factor, band_factor, response, blur_taps, offsets
):
    low_reach = (W + DEC - 1) // DEC
    columns = lax.all_gather(col_factor, "row", axis=1, tiled=True)
    column_wide = extended(columns, (("col", 0),), W)
    coarse_columns = blur_down(column_wide, blur_taps, offsets, columns.shape[0] // DEC)
    merged = jnp.dot(response, band_factor, precision=FULL_PRECISION)
    multi_pairs = (merged[:, None, :] * columns.astype(jnp.float32)[None, :, :]).astype(
        jnp.bfloat16
    )
    hyper_pairs = (band_factor[:, None, :] * coarse_columns[None, :, :]).astype(jnp.bfloat16)
    multi_part = jnp.einsum(
        "kij,kjr->ir", multispectral, multi_pairs, preferred_element_type=jnp.float32
    )
    hyper_part = jnp.einsum(
        "kij,kjr->ir", hyperspectral, hyper_pairs, preferred_element_type=jnp.float32
    )
    column_part = jnp.einsum("jr,js->rs", columns, columns, preferred_element_type=jnp.float32)
    coarse_part = jnp.einsum("jr,js->rs", coarse_columns, coarse_columns, precision=FULL_PRECISION)
    column_gram, coarse_gram = lax.psum((column_part, coarse_part), "col")
    band_gram = jnp.dot(band_factor.T, band_factor, precision=FULL_PRECISION)
    merged_gram = jnp.dot(merged.T, merged, precision=FULL_PRECISION)
    hyper_gram = coarse_gram * band_gram
    multi_gram = column_gram * merged_gram
    cols = lax.axis_size("col")
    multi_blocks = multi_part.reshape(cols, -1, multi_part.shape[1])
    hyper_blocks = hyper_part.reshape(cols, -1, hyper_part.shape[1])
    joined = jnp.concatenate([multi_blocks, hyper_blocks], axis=1)
    joined = lax.psum_scatter(
        joined.reshape(-1, joined.shape[2]), "col", scatter_dimension=0, tiled=True
    )
    multi_sums = joined[: multi_blocks.shape[1]]
    hyper_sums = joined[multi_blocks.shape[1] :]
    start_rows = row_start
    grid = ("row", "col")

    def inner_sum(first_field, second_field):
        return grid_totals([jnp.sum(first_field * second_field)])[0]

    fine_rows = start_rows.shape[0]
    coarse_rows = fine_rows // DEC
    fine_reach = W + DEC * low_reach

    def operate(values):
        fine_wide = extended(values, ((grid, 0),), fine_reach)
        coarse_wide = blur_down(fine_wide, blur_taps, offsets, coarse_rows + 2 * low_reach)
        restored = blur_up(coarse_wide, blur_taps, offsets, low_reach)
        return (
            jnp.dot(restored, hyper_gram, precision=FULL_PRECISION)
            + jnp.dot(values, multi_gram, precision=FULL_PRECISION)
            + RIDGE_TERM * values
        )

    hyper_wide = extended(hyper_sums, ((grid, 0),), low_reach)
    right_side = blur_up(hyper_wide, blur_taps, offsets, low_reach) + multi_sums
    solution = start_rows
    residual = right_side - operate(solution)
    direction = residual
    norm_now = None
    for iteration in range(ITERS):
        mapped = operate(direction)
        if norm_now is None:
            norm_now, curvature = grid_totals(
                [jnp.sum(residual * residual), jnp.sum(direction * mapped)]
            )
        else:
            curvature = inner_sum(direction, mapped)
        step_size = norm_now / curvature
        solution = solution + step_size * direction
        residual = residual - step_size * mapped
        norm_next = inner_sum(residual, residual)
        direction = residual + norm_next / norm_now * direction
        norm_now = norm_next
    return (solution, residual)


def solution(mesh):
    in_specs = (
        P(None, "row", "col"),
        P(None, "row", "col"),
        P(("row", "col"), None),
        P("col", "row"),
        P(),
        P(),
        P(),
        P(),
    )
    out_specs = (P(("row", "col"), None), P(("row", "col"), None))
    return jax.shard_map(body, mesh=mesh, in_specs=in_specs, out_specs=out_specs, check_vma=False)
```

profile of v0, /device:TPU:0, one launch (start us, length us, event | category | flops | bytes accessed | tf_op | source)
XLA Modules:
  0.0 435.6 jit_solution(16213294076576577561)
XLA Ops:
  7.2 25.9 %all_gather.3 = bf16[512,128]{0,1:T(8,128)(2,1)S(1)} all-gather(bf16[512,8]{0,1:T(8,128)(2,1)} %param.11), channel_id=1, replica_groups=mesh['row'=16,'col'=8] {'row'}, dimensions={1}, use_global_device_ids=true | all-gather | bytes 139264 | tf_op jit(solution)/shard_map/all_gather | solution.py:143
  59.2 3.7 fusion.11
  81.8 5.7 %add_bitcast_fusion = f32[128,128]{1,0:T(8,128)S(1)} fusion(bf16[128,1,128]{2,1,0:T(2,128)(2,1)S(1)} %get-tuple-element.69, bf16[128,1,128]{2,1,0:T(2,128)(2,1)S(1)} %get-tuple-element.62, bf16[128,1,128]{2,1,0:T(2,128)(2,1)S(1)} %get-tuple-element.63, bf16[128,1,128]{2,1,0:T(2,128)(2,1)S(1)} %get-tuple-element.64, ...), kind=kLoop, calls=%fused_computation.54 | loop fusion | flops 425984 | bytes 360484 | tf_op jit(solution)/shard_map/add | solution.py:53
  88.5 7.5 %fusion.3 = f32[512,128]{0,1:T(8,128)S(1)} fusion(bf16[96,512,128]{2,1,0:T(8,128)(2,1)} %param.9, f32[128,128]{0,1:T(8,128)S(1)} %copy.203, f32[96,128]{1,0:T(8,128)S(1)} %copy-done.2), kind=kOutput, calls=%fused_computation.5 | convolution fusion | flops 1613758464 | bytes 12959744 | tf_op jit(solution)/shard_map/kij,kjr->ir/dot_general | solution.py:154
  98.4 7.2 %collective-permute-start.5 = (f32[16,128]{1,0:T(8,128)S(1)}, f32[16,128]{1,0:T(8,128)S(1)}, u32[]{:S(2)}, u32[]{:S(2)}) collective-permute-start(f32[16,128]{1,0:T(8,128)S(1)} %get-tuple-element.81), channel_id=1, source_target_pairs={{1,0},{2,1},{3,2},{4,3},{5,4},{6,5},{7,6},{8,7},{9,8},{10,9},{11,1... | collective-permute-start | bytes 24584 | tf_op jit(solution)/shard_map/ppermute | solution.py:33
  173.1 5.7 %fusion.46 = f32[68,1,128]{2,0,1:T(8,128)S(1)} fusion(f32[68,1,128]{2,1,0:T(1,128)S(1)} %get-tuple-element.60, f32[68,1,128]{2,1,0:T(1,128)S(1)} %get-tuple-element.53, f32[68,1,128]{2,1,0:T(1,128)S(1)} %get-tuple-element.54, f32[68,1,128]{2,1,0:T(1,128)S(1)} %get-tuple-element.55, f32[68,1,128]{2,1,0:T(1,128)S(1)} %get-tuple-element.56, ...), kind=kLoop, calls=%fused_computation.125 | loop fusion | flops 147968 | bytes 348196 | tf_op jit(solution)/shard_map/add | solution.py:53
  180.6 25.9 %reduce-scatter.2.cloned.1.call-done = f32[320,128]{1,0:T(8,128)} async-done(((f32[2560,128]{1,0:T(8,128)}), f32[320,128]{1,0:T(8,128)}) %reduce-scatter.2.cloned.1.call-update) | async-done | bytes 163856 | tf_op jit(solution)/shard_map/reduce_scatter | solution.py:168
  207.2 7.2 %collective-permute-start.3 = (f32[2,128]{1,0:T(2,128)S(1)}, f32[2,128]{1,0:T(2,128)S(1)}, u32[]{:S(2)}, u32[]{:S(2)}) collective-permute-start(f32[2,128]{1,0:T(2,128)S(1)} %get-tuple-element.15), channel_id=1, source_target_pairs={{1,0},{2,1},{3,2},{4,3},{5,4},{6,5},{7,6},{8,7},{9,8},{10,9},{11,1... | collective-permute-start | bytes 3080 | tf_op jit(solution)/shard_map/ppermute | solution.py:33
  217.9 7.2 %collective-permute-start.7 = (f32[16,128]{1,0:T(8,128)S(1)}, f32[16,128]{1,0:T(8,128)S(1)}, u32[]{:S(2)}, u32[]{:S(2)}) collective-permute-start(f32[16,128]{1,0:T(8,128)S(1)} %get-tuple-element.77), channel_id=1, source_target_pairs={{1,0},{2,1},{3,2},{4,3},{5,4},{6,5},{7,6},{8,7},{9,8},{10,9},{11,1... | collective-permute-start | bytes 24584 | tf_op jit(solution)/shard_map/ppermute | solution.py:33
  226.8 5.7 %fusion.38 = f32[68,1,128]{2,0,1:T(8,128)S(1)} fusion(f32[68,1,128]{2,1,0:T(1,128)S(1)} %get-tuple-element.51, f32[68,1,128]{2,1,0:T(1,128)S(1)} %get-tuple-element.44, f32[68,1,128]{2,1,0:T(1,128)S(1)} %get-tuple-element.45, f32[68,1,128]{2,1,0:T(1,128)S(1)} %get-tuple-element.46, f32[68,1,128]{2,1,0:T(1,128)S(1)} %get-tuple-element.47, ...), kind=kLoop, calls=%fused_computation.108 | loop fusion | flops 147968 | bytes 348196 | tf_op jit(solution)/shard_map/add | solution.py:53
  236.0 15.1 %shard_map.95 = f32[8,128]{1,0:T(8,128)} custom-call(f32[8,128]{1,0:T(8,128)} %broadcast_in_dim.16.part_ref), custom_call_target="tpu_custom_call" | custom-call | tf_op jit(solution)/shard_map/pallas_call | solution.py:123
  255.7 13.5 %shard_map.96 = f32[8,128]{1,0:T(8,128)} custom-call(f32[8,128]{1,0:T(8,128)} %broadcast_in_dim.17.part_ref), custom_call_target="tpu_custom_call" | custom-call | tf_op jit(solution)/shard_map/pallas_call | solution.py:123
  272.6 6.4 %collective-permute-start.9 = (f32[16,128]{1,0:T(8,128)S(1)}, f32[16,128]{1,0:T(8,128)S(1)}, u32[]{:S(2)}, u32[]{:S(2)}) collective-permute-start(f32[16,128]{1,0:T(8,128)S(1)} %get-tuple-element.75), channel_id=1, source_target_pairs={{1,0},{2,1},{3,2},{4,3},{5,4},{6,5},{7,6},{8,7},{9,8},{10,9},{11,1... | collective-permute-start | bytes 24584 | tf_op jit(solution)/shard_map/ppermute | solution.py:33
  280.7 5.7 %fusion.30 = f32[68,1,128]{2,0,1:T(8,128)S(1)} fusion(f32[68,1,128]{2,1,0:T(1,128)S(1)} %get-tuple-element.42, f32[68,1,128]{2,1,0:T(1,128)S(1)} %get-tuple-element.35, f32[68,1,128]{2,1,0:T(1,128)S(1)} %get-tuple-element.36, f32[68,1,128]{2,1,0:T(1,128)S(1)} %get-tuple-element.37, f32[68,1,128]{2,1,0:T(1,128)S(1)} %get-tuple-element.38, ...), kind=kLoop, calls=%fused_computation.91 | loop fusion | flops 147968 | bytes 348196 | tf_op jit(solution)/shard_map/add | solution.py:53
  289.2 15.1 %shard_map.97 = f32[8,128]{1,0:T(8,128)} custom-call(f32[8,128]{1,0:T(8,128)} %broadcast_in_dim.18.part_ref), custom_call_target="tpu_custom_call" | custom-call | tf_op jit(solution)/shard_map/pallas_call | solution.py:123
  308.6 13.5 %shard_map.98 = f32[8,128]{1,0:T(8,128)} custom-call(f32[8,128]{1,0:T(8,128)} %broadcast_in_dim.19.part_ref), custom_call_target="tpu_custom_call" | custom-call | tf_op jit(solution)/shard_map/pallas_call | solution.py:123
  325.5 6.4 %collective-permute-start.11 = (f32[16,128]{1,0:T(8,128)S(1)}, f32[16,128]{1,0:T(8,128)S(1)}, u32[]{:S(2)}, u32[]{:S(2)}) collective-permute-start(f32[16,128]{1,0:T(8,128)S(1)} %get-tuple-element.73), channel_id=1, source_target_pairs={{1,0},{2,1},{3,2},{4,3},{5,4},{6,5},{7,6},{8,7},{9,8},{10,9},{11,1... | collective-permute-start | bytes 24584 | tf_op jit(solution)/shard_map/ppermute | solution.py:33
  333.6 5.7 %fusion.22 = f32[68,1,128]{2,0,1:T(8,128)S(1)} fusion(f32[68,1,128]{2,1,0:T(1,128)S(1)} %get-tuple-element.33, f32[68,1,128]{2,1,0:T(1,128)S(1)} %get-tuple-element.26, f32[68,1,128]{2,1,0:T(1,128)S(1)} %get-tuple-element.27, f32[68,1,128]{2,1,0:T(1,128)S(1)} %get-tuple-element.28, f32[68,1,128]{2,1,0:T(1,128)S(1)} %get-tuple-element.29, ...), kind=kLoop, calls=%fused_computation.74 | loop fusion | flops 147968 | bytes 348196 | tf_op jit(solution)/shard_map/add | solution.py:53
  342.1 15.1 %shard_map.99 = f32[8,128]{1,0:T(8,128)} custom-call(f32[8,128]{1,0:T(8,128)} %broadcast_in_dim.20.part_ref), custom_call_target="tpu_custom_call" | custom-call | tf_op jit(solution)/shard_map/pallas_call | solution.py:123
  361.6 13.5 %shard_map.100 = f32[8,128]{1,0:T(8,128)} custom-call(f32[8,128]{1,0:T(8,128)} %broadcast_in_dim.21.part_ref), custom_call_target="tpu_custom_call" | custom-call | tf_op jit(solution)/shard_map/pallas_call | solution.py:123
  378.6 6.4 %collective-permute-start.13 = (f32[16,128]{1,0:T(8,128)S(1)}, f32[16,128]{1,0:T(8,128)S(1)}, u32[]{:S(2)}, u32[]{:S(2)}) collective-permute-start(f32[16,128]{1,0:T(8,128)S(1)} %get-tuple-element.71), channel_id=1, source_target_pairs={{1,0},{2,1},{3,2},{4,3},{5,4},{6,5},{7,6},{8,7},{9,8},{10,9},{11,1... | collective-permute-start | bytes 24584 | tf_op jit(solution)/shard_map/ppermute | solution.py:33
  386.7 5.7 %fusion.14 = f32[68,1,128]{2,0,1:T(8,128)S(1)} fusion(f32[68,1,128]{2,1,0:T(1,128)S(1)} %get-tuple-element.24, f32[68,1,128]{2,1,0:T(1,128)S(1)} %get-tuple-element.17, f32[68,1,128]{2,1,0:T(1,128)S(1)} %get-tuple-element.18, f32[68,1,128]{2,1,0:T(1,128)S(1)} %get-tuple-element.19, f32[68,1,128]{2,1,0:T(1,128)S(1)} %get-tuple-element.20, ...), kind=kLoop, calls=%fused_computation.57 | loop fusion | flops 147968 | bytes 348196 | tf_op jit(solution)/shard_map/add | solution.py:53
  395.2 15.1 %shard_map.101 = f32[8,128]{1,0:T(8,128)} custom-call(f32[8,128]{1,0:T(8,128)} %broadcast_in_dim.22.part_ref), custom_call_target="tpu_custom_call" | custom-call | tf_op jit(solution)/shard_map/pallas_call | solution.py:123
  415.3 13.5 %shard_map.102 = f32[8,128]{1,0:T(8,128)} custom-call(f32[8,128]{1,0:T(8,128)} %broadcast_in_dim.23.part_ref), custom_call_target="tpu_custom_call" | custom-call | tf_op jit(solution)/shard_map/pallas_call | solution.py:123
  (147 shorter events, 59.1 us)
Async XLA Ops:
  7.2 51.1 %copy-start = (f32[2,96]{1,0:T(2,128)S(1)}, f32[2,96]{1,0:T(2,128)}, u32[]{:S(2)}) copy-start(f32[2,96]{1,0:T(2,128)} %param.13) | copy-start | bytes 2308
  7.2 172.0 %all-reduce.11.cloned.1.call-start = ((), (), s32[]{:S(2)}) async-start(), calls=%async_computation.2 | async-start | bytes 262144 | tf_op jit(solution)/shard_map/psum | solution.py:159
  33.3 47.8 %collective-permute-start = (bf16[8,128]{1,0:T(8,128)(2,1)S(1)}, bf16[8,128]{1,0:T(8,128)(2,1)S(1)}, u32[]{:S(2)}, u32[]{:S(2)}) collective-permute-start(bf16[8,128]{1,0:T(8,128)(2,1)S(1)} %get-tuple-element.78), channel_id=1, source_target_pairs={{0,1},{1,2},{2,3},{3,4},{4,5},{5,6},{6,7},{7,0},{8,9},{9,10},{10,1... | collective-permute-start | bytes 6152 | tf_op jit(solution)/shard_map/ppermute | solution.py:31
  34.8 46.2 %collective-permute-start.1 = (bf16[8,128]{1,0:T(8,128)(2,1)S(1)}, bf16[8,128]{1,0:T(8,128)(2,1)S(1)}, u32[]{:S(2)}, u32[]{:S(2)}) collective-permute-start(bf16[8,128]{1,0:T(8,128)(2,1)S(1)} %get-tuple-element.79), channel_id=1, source_target_pairs={{1,0},{2,1},{3,2},{4,3},{5,4},{6,5},{7,6},{0,7},{9,8},{10,9},{11,1... | collective-permute-start | bytes 6152 | tf_op jit(solution)/shard_map/ppermute | solution.py:33
  59.2 29.4 %copy-start.2 = (f32[96,128]{1,0:T(8,128)S(1)}, f32[96,128]{1,0:T(8,128)}, u32[]{:S(2)}) copy-start(f32[96,128]{1,0:T(8,128)} %param.12) | copy-start | bytes 147460
  96.2 2.1 copy-start.1
  96.5 110.0 %reduce-scatter.2.cloned.1.call-start = ((), (), s32[]{:S(2)}) async-start(), calls=%async_computation.1 | async-start | bytes 1474560 | tf_op jit(solution)/shard_map/reduce_scatter | solution.py:168
  98.3 74.4 %collective-permute-start.4 = (f32[16,128]{1,0:T(8,128)S(1)}, f32[16,128]{1,0:T(8,128)S(1)}, u32[]{:S(2)}, u32[]{:S(2)}) collective-permute-start(f32[16,128]{1,0:T(8,128)S(1)} %get-tuple-element.80), channel_id=1, source_target_pairs={{0,1},{1,2},{2,3},{3,4},{4,5},{5,6},{6,7},{7,8},{8,9},{9,10},{10,1... | collective-permute-start | bytes 24584 | tf_op jit(solution)/shard_map/ppermute | solution.py:31
  98.4 74.3 %collective-permute-start.5 = (f32[16,128]{1,0:T(8,128)S(1)}, f32[16,128]{1,0:T(8,128)S(1)}, u32[]{:S(2)}, u32[]{:S(2)}) collective-permute-start(f32[16,128]{1,0:T(8,128)S(1)} %get-tuple-element.81), channel_id=1, source_target_pairs={{1,0},{2,1},{3,2},{4,3},{5,4},{6,5},{7,6},{8,7},{9,8},{10,9},{11,1... | collective-permute-start | bytes 24584 | tf_op jit(solution)/shard_map/ppermute | solution.py:33
  207.2 9.1 %collective-permute-start.2 = (f32[2,128]{1,0:T(2,128)S(1)}, f32[2,128]{1,0:T(2,128)S(1)}, u32[]{:S(2)}, u32[]{:S(2)}) collective-permute-start(f32[2,128]{1,0:T(2,128)S(1)} %get-tuple-element.14), channel_id=1, source_target_pairs={{0,1},{1,2},{2,3},{3,4},{4,5},{5,6},{6,7},{7,8},{8,9},{9,10},{10,1... | collective-permute-start | bytes 3080 | tf_op jit(solution)/shard_map/ppermute | solution.py:31
  207.2 9.1 %collective-permute-start.3 = (f32[2,128]{1,0:T(2,128)S(1)}, f32[2,128]{1,0:T(2,128)S(1)}, u32[]{:S(2)}, u32[]{:S(2)}) collective-permute-start(f32[2,128]{1,0:T(2,128)S(1)} %get-tuple-element.15), channel_id=1, source_target_pairs={{1,0},{2,1},{3,2},{4,3},{5,4},{6,5},{7,6},{8,7},{9,8},{10,9},{11,1... | collective-permute-start | bytes 3080 | tf_op jit(solution)/shard_map/ppermute | solution.py:33
  217.9 8.6 %collective-permute-start.6 = (f32[16,128]{1,0:T(8,128)S(1)}, f32[16,128]{1,0:T(8,128)S(1)}, u32[]{:S(2)}, u32[]{:S(2)}) collective-permute-start(f32[16,128]{1,0:T(8,128)S(1)} %get-tuple-element.76), channel_id=1, source_target_pairs={{0,1},{1,2},{2,3},{3,4},{4,5},{5,6},{6,7},{7,8},{8,9},{9,10},{10,1... | collective-permute-start | bytes 24584 | tf_op jit(solution)/shard_map/ppermute | solution.py:31
  217.9 8.5 %collective-permute-start.7 = (f32[16,128]{1,0:T(8,128)S(1)}, f32[16,128]{1,0:T(8,128)S(1)}, u32[]{:S(2)}, u32[]{:S(2)}) collective-permute-start(f32[16,128]{1,0:T(8,128)S(1)} %get-tuple-element.77), channel_id=1, source_target_pairs={{1,0},{2,1},{3,2},{4,3},{5,4},{6,5},{7,6},{8,7},{9,8},{10,9},{11,1... | collective-permute-start | bytes 24584 | tf_op jit(solution)/shard_map/ppermute | solution.py:33
  271.7 8.6 %collective-permute-start.8 = (f32[16,128]{1,0:T(8,128)S(1)}, f32[16,128]{1,0:T(8,128)S(1)}, u32[]{:S(2)}, u32[]{:S(2)}) collective-permute-start(f32[16,128]{1,0:T(8,128)S(1)} %get-tuple-element.74), channel_id=1, source_target_pairs={{0,1},{1,2},{2,3},{3,4},{4,5},{5,6},{6,7},{7,8},{8,9},{9,10},{10,1... | collective-permute-start | bytes 24584 | tf_op jit(solution)/shard_map/ppermute | solution.py:31
  272.6 7.7 %collective-permute-start.9 = (f32[16,128]{1,0:T(8,128)S(1)}, f32[16,128]{1,0:T(8,128)S(1)}, u32[]{:S(2)}, u32[]{:S(2)}) collective-permute-start(f32[16,128]{1,0:T(8,128)S(1)} %get-tuple-element.75), channel_id=1, source_target_pairs={{1,0},{2,1},{3,2},{4,3},{5,4},{6,5},{7,6},{8,7},{9,8},{10,9},{11,1... | collective-permute-start | bytes 24584 | tf_op jit(solution)/shard_map/ppermute | solution.py:33
  324.6 8.6 %collective-permute-start.10 = (f32[16,128]{1,0:T(8,128)S(1)}, f32[16,128]{1,0:T(8,128)S(1)}, u32[]{:S(2)}, u32[]{:S(2)}) collective-permute-start(f32[16,128]{1,0:T(8,128)S(1)} %get-tuple-element.72), channel_id=1, source_target_pairs={{0,1},{1,2},{2,3},{3,4},{4,5},{5,6},{6,7},{7,8},{8,9},{9,10},{10,1... | collective-permute-start | bytes 24584 | tf_op jit(solution)/shard_map/ppermute | solution.py:31
  325.5 7.7 %collective-permute-start.11 = (f32[16,128]{1,0:T(8,128)S(1)}, f32[16,128]{1,0:T(8,128)S(1)}, u32[]{:S(2)}, u32[]{:S(2)}) collective-permute-start(f32[16,128]{1,0:T(8,128)S(1)} %get-tuple-element.73), channel_id=1, source_target_pairs={{1,0},{2,1},{3,2},{4,3},{5,4},{6,5},{7,6},{8,7},{9,8},{10,9},{11,1... | collective-permute-start | bytes 24584 | tf_op jit(solution)/shard_map/ppermute | solution.py:33
  377.7 8.6 %collective-permute-start.12 = (f32[16,128]{1,0:T(8,128)S(1)}, f32[16,128]{1,0:T(8,128)S(1)}, u32[]{:S(2)}, u32[]{:S(2)}) collective-permute-start(f32[16,128]{1,0:T(8,128)S(1)} %get-tuple-element.70), channel_id=1, source_target_pairs={{0,1},{1,2},{2,3},{3,4},{4,5},{5,6},{6,7},{7,8},{8,9},{9,10},{10,1... | collective-permute-start | bytes 24584 | tf_op jit(solution)/shard_map/ppermute | solution.py:31
  378.6 7.7 %collective-permute-start.13 = (f32[16,128]{1,0:T(8,128)S(1)}, f32[16,128]{1,0:T(8,128)S(1)}, u32[]{:S(2)}, u32[]{:S(2)}) collective-permute-start(f32[16,128]{1,0:T(8,128)S(1)} %get-tuple-element.71), channel_id=1, source_target_pairs={{1,0},{2,1},{3,2},{4,3},{5,4},{6,5},{7,6},{8,7},{9,8},{10,9},{11,1... | collective-permute-start | bytes 24584 | tf_op jit(solution)/shard_map/ppermute | solution.py:33
Sparse Core Ops, SparseCore 0:
  96.6 68.0 all-reduce.10
  167.2 39.1 reduce-scatter.1
where the time goes:
time: 440 us; the launch traced here: 436 us
  between operations  124 us (28%)
  Pallas kernels  115 us (26%)
  starting transfers between devices  47.7 us (11%)
  other arithmetic  42.1 us (10%)
  waiting for transfers between devices  31.4 us (7%)
  local copies, waits for them, and re-layouts  27.5 us (6%)
  blocking collectives  25.9 us (6%)
  matrix products  22.1 us (5%)
    pallas_call x8, Pallas kernels, grid_totals(): pl.pallas_call(functools.partial(total_kernel, rows, cols), out_shape=jax...  115 us
    ppermute x7, starting transfers between devices, extended(): lax.ppermute(head, axis, [((i + 1) % count, i) for i in range(count)])  43.2 us
    add x6, other arithmetic, blur_down(): total = total + weights[number] * piece.astype(jnp.float32)  34 us
    all_gather x1, blocking collectives, body(): columns = lax.all_gather(col_factor, 'row', axis=1, tiled=True)  25.9 us
    reduce_scatter x1, waiting for transfers between devices, body(): lax.psum_scatter(joined.reshape(-1, joined.shape[2]), 'col', scatter_dime...  25.9 us
  transfers between devices with their start and end apart: 16, of which 5 were waited for; matrix products, arithmetic and copies ran while one was open for 5% of the time, Pallas kernels for 0%

commit v1 on v0

--- a/solution.py
+++ b/solution.py
@@ -136,6 +136,62 @@
     return [summed[0, number] for number in range(len(parts))]
 
 
+def scatter_kernel(cols, blocks_ref, gram_ref, sums_ref, grams_ref, held, gram_held, sends, receipts):
+    here_row = lax.axis_index("row")
+    here_col = lax.axis_index("col")
+    peers = [lax.rem(here_col + shift, cols) for shift in range(1, cols)]
+    barrier = pltpu.get_barrier_semaphore()
+    for peer in peers:
+        pl.semaphore_signal(barrier, inc=1, device_id=(here_row, peer), device_id_type=MESH)
+    pl.semaphore_wait(barrier, len(peers))
+    copies = []
+    for number, peer in enumerate(peers):
+        for slot, (source, target) in enumerate(
+            ((blocks_ref.at[peer], held.at[here_col]), (gram_ref, gram_held.at[here_col]))
+        ):
+            copy = pltpu.make_async_remote_copy(
+                src_ref=source,
+                dst_ref=target,
+                send_sem=sends.at[2 * number + slot],
+                recv_sem=receipts.at[2 * number + slot],
+                device_id=(here_row, peer),
+                device_id_type=MESH,
+            )
+            copy.start()
+            copies.append(copy)
+    held[here_col] = blocks_ref[here_col]
+    gram_held[here_col] = gram_ref[...]
+    for copy in copies:
+        copy.wait()
+    sums = held[0]
+    grams = gram_held[0]
+    for source in range(1, cols):
+        sums = sums + held[source]
+        grams = grams + gram_held[source]
+    sums_ref[...] = sums
+    grams_ref[...] = grams
+
+
+def col_scatter(blocks, gram):
+    cols = blocks.shape[0]
+    return pl.pallas_call(
+        functools.partial(scatter_kernel, cols),
+        out_shape=(
+            jax.ShapeDtypeStruct(blocks.shape[1:], jnp.float32),
+            jax.ShapeDtypeStruct(gram.shape, jnp.float32),
+        ),
+        in_specs=[pl.BlockSpec(memory_space=pltpu.VMEM)] * 2,
+        out_specs=(pl.BlockSpec(memory_space=pltpu.VMEM),) * 2,
+        scratch_shapes=[
+            pltpu.VMEM(blocks.shape, jnp.float32),
+            pltpu.VMEM((cols,) + gram.shape, jnp.float32),
+            pltpu.SemaphoreType.DMA((2 * cols,)),
+            pltpu.SemaphoreType.DMA((2 * cols,)),
+        ],
+        compiler_params=pltpu.CompilerParams(collective_id=1, has_side_effects=True),
+    )(blocks, gram)
+
+
 def body(
     multispectral, hyperspectral, row_start, col_factor, band_factor, response, blur_taps, offsets
 ):
@@ -156,18 +212,17 @@
     )
     column_part = jnp.einsum("jr,js->rs", columns, columns, preferred_element_type=jnp.float32)
     coarse_part = jnp.einsum("jr,js->rs", coarse_columns, coarse_columns, precision=FULL_PRECISION)
-    column_gram, coarse_gram = lax.psum((column_part, coarse_part), "col")
+    cols = lax.axis_size("col")
+    multi_blocks = multi_part.reshape(cols, -1, multi_part.shape[1])
+    hyper_blocks = hyper_part.reshape(cols, -1, hyper_part.shape[1])
+    joined = jnp.concatenate([multi_blocks, hyper_blocks], axis=1)
+    joined, gram_sums = col_scatter(joined, jnp.concatenate([column_part, coarse_part], axis=0))
+    column_gram = gram_sums[: column_part.shape[0]]
+    coarse_gram = gram_sums[column_part.shape[0] :]
     band_gram = jnp.dot(band_factor.T, band_factor, precision=FULL_PRECISION)
     merged_gram = jnp.dot(merged.T, merged, precision=FULL_PRECISION)
     hyper_gram = coarse_gram * band_gram
     multi_gram = column_gram * merged_gram
-    cols = lax.axis_size("col")
-    multi_blocks = multi_part.reshape(cols, -1, multi_part.shape[1])
-    hyper_blocks = hyper_part.reshape(cols, -1, hyper_part.shape[1])
-    joined = jnp.concatenate([multi_blocks, hyper_blocks], axis=1)
-    joined = lax.psum_scatter(
-        joined.reshape(-1, joined.shape[2]), "col", scatter_dimension=0, tiled=True
-    )
     multi_sums = joined[: multi_blocks.shape[1]]
     hyper_sums = joined[multi_blocks.shape[1] :]
     start_rows = row_start

time: 440 us -> 431 us (0.980)
  Pallas kernels: 115 us -> 145 us
  waiting for transfers between devices: 31.4 us -> 5.48 us
  between operations: 124 us -> 113 us
    pallas_call x0 -> x1, Pallas kernels: none -> 30.3 us  [col_scatter(): pl.pallas_call(functools.partial(scatter_kernel, cols), out_shape=(jax.Sh...]
    reduce_scatter x1 -> x0, waiting for transfers between devices: 25.9 us -> none  [body(): lax.psum_scatter(joined.reshape(-1, joined.shape[2]), 'col', scatter_dime...]
  transfers between devices with their start and end apart: 16 -> 14, of which waited for: 5 -> 4; matrix products, arithmetic and copies ran while one was open for 5% -> 7% of each run, Pallas kernels for 0% -> 7%
where the time goes in v1:
time: 431 us; the launch traced here: 427 us
  Pallas kernels  145 us (34%)
  between operations  113 us (26%)
  starting transfers between devices  47.5 us (11%)
  other arithmetic  43.8 us (10%)
  local copies, waits for them, and re-layouts  26.4 us (6%)
  blocking collectives  25.9 us (6%)
  matrix products  19.9 us (5%)
  waiting for transfers between devices  5.48 us (1%)
    pallas_call x8, Pallas kernels, grid_totals(): pl.pallas_call(functools.partial(total_kernel, rows, cols), out_shape=jax...  115 us
    ppermute x7, starting transfers between devices, extended(): lax.ppermute(head, axis, [((i + 1) % count, i) for i in range(count)])  43.3 us
    add x6, other arithmetic, blur_down(): total = total + weights[number] * piece.astype(jnp.float32)  34 us
    pallas_call x1, Pallas kernels, col_scatter(): pl.pallas_call(functools.partial(scatter_kernel, cols), out_shape=(jax.Sh...  30.3 us
    all_gather x1, blocking collectives, body(): columns = lax.all_gather(col_factor, 'row', axis=1, tiled=True)  25.9 us
  transfers between devices with their start and end apart: 14, of which 4 were waited for; matrix products, arithmetic and copies ran while one was open for 7% of the time, Pallas kernels for 7%

profile of v1, /device:TPU:0, one launch (start us, length us, event | category | flops | bytes accessed | tf_op | source)
XLA Modules:
  0.0 427.1 jit_solution(9719076578819158350)
XLA Ops:
  0.6 25.9 %all_gather.3 = bf16[512,128]{0,1:T(8,128)(2,1)S(1)} all-gather(bf16[512,8]{0,1:T(8,128)(2,1)} %param.11), channel_id=1, replica_groups=mesh['row'=16,'col'=8] {'row'}, dimensions={1}, use_global_device_ids=true | all-gather | bytes 139264 | tf_op jit(solution)/shard_map/all_gather | solution.py:199
  31.6 7.2 %collective-permute-start.5 = (f32[16,128]{1,0:T(8,128)S(1)}, f32[16,128]{1,0:T(8,128)S(1)}, u32[]{:S(2)}, u32[]{:S(2)}) collective-permute-start(f32[16,128]{1,0:T(8,128)S(1)} %get-tuple-element.83), channel_id=1, source_target_pairs={{1,0},{2,1},{3,2},{4,3},{5,4},{6,5},{7,6},{8,7},{9,8},{10,9},{11,1... | collective-permute-start | bytes 24584 | tf_op jit(solution)/shard_map/ppermute | solution.py:33
  107.0 3.7 convolution_bitcast_fusion
  151.6 5.7 %add_bitcast_fusion = f32[128,128]{1,0:T(8,128)S(1)} fusion(bf16[128,1,128]{2,1,0:T(2,128)(2,1)S(1)} %get-tuple-element.71, bf16[128,1,128]{2,1,0:T(2,128)(2,1)S(1)} %get-tuple-element.64, bf16[128,1,128]{2,1,0:T(2,128)(2,1)S(1)} %get-tuple-element.65, bf16[128,1,128]{2,1,0:T(2,128)(2,1)S(1)} %get-tuple-element.66, ...), kind=kLoop, calls=%fused_computation.54 | loop fusion | flops 425984 | bytes 360484 | tf_op jit(solution)/shard_map/add | solution.py:53
  157.7 7.5 %fusion.3 = f32[512,128]{0,1:T(8,128)S(1)} fusion(bf16[96,512,128]{2,1,0:T(8,128)(2,1)} %param.9, f32[128,128]{0,1:T(8,128)S(1)} %copy.204, f32[96,128]{1,0:T(8,128)S(1)} %copy-done.2), kind=kOutput, calls=%fused_computation.6 | convolution fusion | flops 1613758464 | bytes 12959744 | tf_op jit(solution)/shard_map/kij,kjr->ir/dot_general | solution.py:210
  167.2 30.3 %shard_map.95 = (f32[320,128]{1,0:T(8,128)}, f32[256,128]{1,0:T(8,128)}) custom-call(f32[8,320,128]{2,1,0:T(8,128)} %pad_maximum_fusion.blocks_ref, f32[256,128]{1,0:T(8,128)} %pad_maximum_fusion.7.gram_ref), custom_call_target="tpu_custom_call" | custom-call | tf_op jit(solution)/shard_map/pallas_call | solution.py:177
  198.3 7.2 %collective-permute-start.3 = (f32[2,128]{1,0:T(2,128)S(1)}, f32[2,128]{1,0:T(2,128)S(1)}, u32[]{:S(2)}, u32[]{:S(2)}) collective-permute-start(f32[2,128]{1,0:T(2,128)S(1)} %get-tuple-element.17), channel_id=1, source_target_pairs={{1,0},{2,1},{3,2},{4,3},{5,4},{6,5},{7,6},{8,7},{9,8},{10,9},{11,1... | collective-permute-start | bytes 3080 | tf_op jit(solution)/shard_map/ppermute | solution.py:33
  209.3 5.7 %fusion.45 = f32[68,1,128]{2,0,1:T(8,128)S(1)} fusion(f32[68,1,128]{2,1,0:T(1,128)S(1)} %get-tuple-element.62, f32[68,1,128]{2,1,0:T(1,128)S(1)} %get-tuple-element.55, f32[68,1,128]{2,1,0:T(1,128)S(1)} %get-tuple-element.56, f32[68,1,128]{2,1,0:T(1,128)S(1)} %get-tuple-element.57, f32[68,1,128]{2,1,0:T(1,128)S(1)} %get-tuple-element.58, ...), kind=kLoop, calls=%fused_computation.125 | loop fusion | flops 147968 | bytes 348196 | tf_op jit(solution)/shard_map/add | solution.py:53
  216.0 7.2 %collective-permute-start.7 = (f32[16,128]{1,0:T(8,128)S(1)}, f32[16,128]{1,0:T(8,128)S(1)}, u32[]{:S(2)}, u32[]{:S(2)}) collective-permute-start(f32[16,128]{1,0:T(8,128)S(1)} %get-tuple-element.79), channel_id=1, source_target_pairs={{1,0},{2,1},{3,2},{4,3},{5,4},{6,5},{7,6},{8,7},{9,8},{10,9},{11,1... | collective-permute-start | bytes 24584 | tf_op jit(solution)/shard_map/ppermute | solution.py:33
  224.9 5.7 %fusion.37 = f32[68,1,128]{2,0,1:T(8,128)S(1)} fusion(f32[68,1,128]{2,1,0:T(1,128)S(1)} %get-tuple-element.53, f32[68,1,128]{2,1,0:T(1,128)S(1)} %get-tuple-element.46, f32[68,1,128]{2,1,0:T(1,128)S(1)} %get-tuple-element.47, f32[68,1,128]{2,1,0:T(1,128)S(1)} %get-tuple-element.48, f32[68,1,128]{2,1,0:T(1,128)S(1)} %get-tuple-element.49, ...), kind=kLoop, calls=%fused_computation.108 | loop fusion | flops 147968 | bytes 348196 | tf_op jit(solution)/shard_map/add | solution.py:53
  234.1 15.1 %shard_map.96 = f32[8,128]{1,0:T(8,128)} custom-call(f32[8,128]{1,0:T(8,128)} %broadcast_in_dim.16.part_ref), custom_call_target="tpu_custom_call" | custom-call | tf_op jit(solution)/shard_map/pallas_call | solution.py:123
  253.8 13.5 %shard_map.97 = f32[8,128]{1,0:T(8,128)} custom-call(f32[8,128]{1,0:T(8,128)} %broadcast_in_dim.17.part_ref), custom_call_target="tpu_custom_call" | custom-call | tf_op jit(solution)/shard_map/pallas_call | solution.py:123
  270.7 6.4 %collective-permute-start.9 = (f32[16,128]{1,0:T(8,128)S(1)}, f32[16,128]{1,0:T(8,128)S(1)}, u32[]{:S(2)}, u32[]{:S(2)}) collective-permute-start(f32[16,128]{1,0:T(8,128)S(1)} %get-tuple-element.77), channel_id=1, source_target_pairs={{1,0},{2,1},{3,2},{4,3},{5,4},{6,5},{7,6},{8,7},{9,8},{10,9},{11,1... | collective-permute-start | bytes 24584 | tf_op jit(solution)/shard_map/ppermute | solution.py:33
  278.8 5.7 %fusion.29 = f32[68,1,128]{2,0,1:T(8,128)S(1)} fusion(f32[68,1,128]{2,1,0:T(1,128)S(1)} %get-tuple-element.44, f32[68,1,128]{2,1,0:T(1,128)S(1)} %get-tuple-element.37, f32[68,1,128]{2,1,0:T(1,128)S(1)} %get-tuple-element.38, f32[68,1,128]{2,1,0:T(1,128)S(1)} %get-tuple-element.39, f32[68,1,128]{2,1,0:T(1,128)S(1)} %get-tuple-element.40, ...), kind=kLoop, calls=%fused_computation.91 | loop fusion | flops 147968 | bytes 348196 | tf_op jit(solution)/shard_map/add | solution.py:53
  287.3 15.1 %shard_map.98 = f32[8,128]{1,0:T(8,128)} custom-call(f32[8,128]{1,0:T(8,128)} %broadcast_in_dim.18.part_ref), custom_call_target="tpu_custom_call" | custom-call | tf_op jit(solution)/shard_map/pallas_call | solution.py:123
  306.7 13.5 %shard_map.99 = f32[8,128]{1,0:T(8,128)} custom-call(f32[8,128]{1,0:T(8,128)} %broadcast_in_dim.19.part_ref), custom_call_target="tpu_custom_call" | custom-call | tf_op jit(solution)/shard_map/pallas_call | solution.py:123
  323.6 6.4 %collective-permute-start.11 = (f32[16,128]{1,0:T(8,128)S(1)}, f32[16,128]{1,0:T(8,128)S(1)}, u32[]{:S(2)}, u32[]{:S(2)}) collective-permute-start(f32[16,128]{1,0:T(8,128)S(1)} %get-tuple-element.75), channel_id=1, source_target_pairs={{1,0},{2,1},{3,2},{4,3},{5,4},{6,5},{7,6},{8,7},{9,8},{10,9},{11,1... | collective-permute-start | bytes 24584 | tf_op jit(solution)/shard_map/ppermute | solution.py:33
  331.7 5.7 %fusion.21 = f32[68,1,128]{2,0,1:T(8,128)S(1)} fusion(f32[68,1,128]{2,1,0:T(1,128)S(1)} %get-tuple-element.35, f32[68,1,128]{2,1,0:T(1,128)S(1)} %get-tuple-element.28, f32[68,1,128]{2,1,0:T(1,128)S(1)} %get-tuple-element.29, f32[68,1,128]{2,1,0:T(1,128)S(1)} %get-tuple-element.30, f32[68,1,128]{2,1,0:T(1,128)S(1)} %get-tuple-element.31, ...), kind=kLoop, calls=%fused_computation.74 | loop fusion | flops 147968 | bytes 348196 | tf_op jit(solution)/shard_map/add | solution.py:53
  340.2 15.1 %shard_map.100 = f32[8,128]{1,0:T(8,128)} custom-call(f32[8,128]{1,0:T(8,128)} %broadcast_in_dim.20.part_ref), custom_call_target="tpu_custom_call" | custom-call | tf_op jit(solution)/shard_map/pallas_call | solution.py:123
  359.7 13.5 %shard_map.101 = f32[8,128]{1,0:T(8,128)} custom-call(f32[8,128]{1,0:T(8,128)} %broadcast_in_dim.21.part_ref), custom_call_target="tpu_custom_call" | custom-call | tf_op jit(solution)/shard_map/pallas_call | solution.py:123
  376.7 6.4 %collective-permute-start.13 = (f32[16,128]{1,0:T(8,128)S(1)}, f32[16,128]{1,0:T(8,128)S(1)}, u32[]{:S(2)}, u32[]{:S(2)}) collective-permute-start(f32[16,128]{1,0:T(8,128)S(1)} %get-tuple-element.73), channel_id=1, source_target_pairs={{1,0},{2,1},{3,2},{4,3},{5,4},{6,5},{7,6},{8,7},{9,8},{10,9},{11,1... | collective-permute-start | bytes 24584 | tf_op jit(solution)/shard_map/ppermute | solution.py:33
  384.7 5.7 %fusion.13 = f32[68,1,128]{2,0,1:T(8,128)S(1)} fusion(f32[68,1,128]{2,1,0:T(1,128)S(1)} %get-tuple-element.26, f32[68,1,128]{2,1,0:T(1,128)S(1)} %get-tuple-element.19, f32[68,1,128]{2,1,0:T(1,128)S(1)} %get-tuple-element.20, f32[68,1,128]{2,1,0:T(1,128)S(1)} %get-tuple-element.21, f32[68,1,128]{2,1,0:T(1,128)S(1)} %get-tuple-element.22, ...), kind=kLoop, calls=%fused_computation.57 | loop fusion | flops 147968 | bytes 348196 | tf_op jit(solution)/shard_map/add | solution.py:53
  393.2 15.1 %shard_map.102 = f32[8,128]{1,0:T(8,128)} custom-call(f32[8,128]{1,0:T(8,128)} %broadcast_in_dim.22.part_ref), custom_call_target="tpu_custom_call" | custom-call | tf_op jit(solution)/shard_map/pallas_call | solution.py:123
  413.4 13.5 %shard_map.103 = f32[8,128]{1,0:T(8,128)} custom-call(f32[8,128]{1,0:T(8,128)} %broadcast_in_dim.23.part_ref), custom_call_target="tpu_custom_call" | custom-call | tf_op jit(solution)/shard_map/pallas_call | solution.py:123
  (143 shorter events, 57.3 us)
Async XLA Ops:
  0.6 105.5 %copy-start = (f32[2,96]{1,0:T(2,128)S(1)}, f32[2,96]{1,0:T(2,128)}, u32[]{:S(2)}) copy-start(f32[2,96]{1,0:T(2,128)} %param.13) | copy-start | bytes 2308
  26.7 124.2 %collective-permute-start = (bf16[8,128]{1,0:T(8,128)(2,1)S(1)}, bf16[8,128]{1,0:T(8,128)(2,1)S(1)}, u32[]{:S(2)}, u32[]{:S(2)}) collective-permute-start(bf16[8,128]{1,0:T(8,128)(2,1)S(1)} %get-tuple-element.80), channel_id=1, source_target_pairs={{0,1},{1,2},{2,3},{3,4},{4,5},{5,6},{6,7},{7,0},{8,9},{9,10},{10,1... | collective-permute-start | bytes 6152 | tf_op jit(solution)/shard_map/ppermute | solution.py:31
  28.3 122.6 %collective-permute-start.1 = (bf16[8,128]{1,0:T(8,128)(2,1)S(1)}, bf16[8,128]{1,0:T(8,128)(2,1)S(1)}, u32[]{:S(2)}, u32[]{:S(2)}) collective-permute-start(bf16[8,128]{1,0:T(8,128)(2,1)S(1)} %get-tuple-element.81), channel_id=1, source_target_pairs={{1,0},{2,1},{3,2},{4,3},{5,4},{6,5},{7,6},{0,7},{9,8},{10,9},{11,1... | collective-permute-start | bytes 6152 | tf_op jit(solution)/shard_map/ppermute | solution.py:33
  31.6 177.3 %collective-permute-start.4 = (f32[16,128]{1,0:T(8,128)S(1)}, f32[16,128]{1,0:T(8,128)S(1)}, u32[]{:S(2)}, u32[]{:S(2)}) collective-permute-start(f32[16,128]{1,0:T(8,128)S(1)} %get-tuple-element.82), channel_id=1, source_target_pairs={{0,1},{1,2},{2,3},{3,4},{4,5},{5,6},{6,7},{7,8},{8,9},{9,10},{10,1... | collective-permute-start | bytes 24584 | tf_op jit(solution)/shard_map/ppermute | solution.py:31
  31.6 177.3 %collective-permute-start.5 = (f32[16,128]{1,0:T(8,128)S(1)}, f32[16,128]{1,0:T(8,128)S(1)}, u32[]{:S(2)}, u32[]{:S(2)}) collective-permute-start(f32[16,128]{1,0:T(8,128)S(1)} %get-tuple-element.83), channel_id=1, source_target_pairs={{1,0},{2,1},{3,2},{4,3},{5,4},{6,5},{7,6},{8,7},{9,8},{10,9},{11,1... | collective-permute-start | bytes 24584 | tf_op jit(solution)/shard_map/ppermute | solution.py:33
  107.0 50.7 %copy-start.2 = (f32[96,128]{1,0:T(8,128)S(1)}, f32[96,128]{1,0:T(8,128)}, u32[]{:S(2)}) copy-start(f32[96,128]{1,0:T(8,128)} %param.12) | copy-start | bytes 147460
  165.2 43.7 %copy-start.1 = (f32[256,128]{1,0:T(8,128)S(1)}, f32[256,128]{1,0:T(8,128)}, u32[]{:S(2)}) copy-start(f32[256,128]{1,0:T(8,128)} %param.10) | copy-start | bytes 393220
  197.5 18.1 %copy-start.3 = (f32[320,128]{1,0:T(8,128)S(1)}, f32[320,128]{1,0:T(8,128)}, u32[]{:S(2)}) copy-start(f32[320,128]{1,0:T(8,128)} %get-tuple-element.4) | copy-start | bytes 491524
  198.3 10.2 %collective-permute-start.2 = (f32[2,128]{1,0:T(2,128)S(1)}, f32[2,128]{1,0:T(2,128)S(1)}, u32[]{:S(2)}, u32[]{:S(2)}) collective-permute-start(f32[2,128]{1,0:T(2,128)S(1)} %get-tuple-element.16), channel_id=1, source_target_pairs={{0,1},{1,2},{2,3},{3,4},{4,5},{5,6},{6,7},{7,8},{8,9},{9,10},{10,1... | collective-permute-start | bytes 3080 | tf_op jit(solution)/shard_map/ppermute | solution.py:31
  198.3 10.2 %collective-permute-start.3 = (f32[2,128]{1,0:T(2,128)S(1)}, f32[2,128]{1,0:T(2,128)S(1)}, u32[]{:S(2)}, u32[]{:S(2)}) collective-permute-start(f32[2,128]{1,0:T(2,128)S(1)} %get-tuple-element.17), channel_id=1, source_target_pairs={{1,0},{2,1},{3,2},{4,3},{5,4},{6,5},{7,6},{8,7},{9,8},{10,9},{11,1... | collective-permute-start | bytes 3080 | tf_op jit(solution)/shard_map/ppermute | solution.py:33
  216.0 8.6 %collective-permute-start.6 = (f32[16,128]{1,0:T(8,128)S(1)}, f32[16,128]{1,0:T(8,128)S(1)}, u32[]{:S(2)}, u32[]{:S(2)}) collective-permute-start(f32[16,128]{1,0:T(8,128)S(1)} %get-tuple-element.78), channel_id=1, source_target_pairs={{0,1},{1,2},{2,3},{3,4},{4,5},{5,6},{6,7},{7,8},{8,9},{9,10},{10,1... | collective-permute-start | bytes 24584 | tf_op jit(solution)/shard_map/ppermute | solution.py:31
  216.0 8.5 %collective-permute-start.7 = (f32[16,128]{1,0:T(8,128)S(1)}, f32[16,128]{1,0:T(8,128)S(1)}, u32[]{:S(2)}, u32[]{:S(2)}) collective-permute-start(f32[16,128]{1,0:T(8,128)S(1)} %get-tuple-element.79), channel_id=1, source_target_pairs={{1,0},{2,1},{3,2},{4,3},{5,4},{6,5},{7,6},{8,7},{9,8},{10,9},{11,1... | collective-permute-start | bytes 24584 | tf_op jit(solution)/shard_map/ppermute | solution.py:33
  269.8 8.6 %collective-permute-start.8 = (f32[16,128]{1,0:T(8,128)S(1)}, f32[16,128]{1,0:T(8,128)S(1)}, u32[]{:S(2)}, u32[]{:S(2)}) collective-permute-start(f32[16,128]{1,0:T(8,128)S(1)} %get-tuple-element.76), channel_id=1, source_target_pairs={{0,1},{1,2},{2,3},{3,4},{4,5},{5,6},{6,7},{7,8},{8,9},{9,10},{10,1... | collective-permute-start | bytes 24584 | tf_op jit(solution)/shard_map/ppermute | solution.py:31
  270.7 7.7 %collective-permute-start.9 = (f32[16,128]{1,0:T(8,128)S(1)}, f32[16,128]{1,0:T(8,128)S(1)}, u32[]{:S(2)}, u32[]{:S(2)}) collective-permute-start(f32[16,128]{1,0:T(8,128)S(1)} %get-tuple-element.77), channel_id=1, source_target_pairs={{1,0},{2,1},{3,2},{4,3},{5,4},{6,5},{7,6},{8,7},{9,8},{10,9},{11,1... | collective-permute-start | bytes 24584 | tf_op jit(solution)/shard_map/ppermute | solution.py:33
  322.7 8.6 %collective-permute-start.10 = (f32[16,128]{1,0:T(8,128)S(1)}, f32[16,128]{1,0:T(8,128)S(1)}, u32[]{:S(2)}, u32[]{:S(2)}) collective-permute-start(f32[16,128]{1,0:T(8,128)S(1)} %get-tuple-element.74), channel_id=1, source_target_pairs={{0,1},{1,2},{2,3},{3,4},{4,5},{5,6},{6,7},{7,8},{8,9},{9,10},{10,1... | collective-permute-start | bytes 24584 | tf_op jit(solution)/shard_map/ppermute | solution.py:31
  323.6 7.7 %collective-permute-start.11 = (f32[16,128]{1,0:T(8,128)S(1)}, f32[16,128]{1,0:T(8,128)S(1)}, u32[]{:S(2)}, u32[]{:S(2)}) collective-permute-start(f32[16,128]{1,0:T(8,128)S(1)} %get-tuple-element.75), channel_id=1, source_target_pairs={{1,0},{2,1},{3,2},{4,3},{5,4},{6,5},{7,6},{8,7},{9,8},{10,9},{11,1... | collective-permute-start | bytes 24584 | tf_op jit(solution)/shard_map/ppermute | solution.py:33
  375.8 8.6 %collective-permute-start.12 = (f32[16,128]{1,0:T(8,128)S(1)}, f32[16,128]{1,0:T(8,128)S(1)}, u32[]{:S(2)}, u32[]{:S(2)}) collective-permute-start(f32[16,128]{1,0:T(8,128)S(1)} %get-tuple-element.72), channel_id=1, source_target_pairs={{0,1},{1,2},{2,3},{3,4},{4,5},{5,6},{6,7},{7,8},{8,9},{9,10},{10,1... | collective-permute-start | bytes 24584 | tf_op jit(solution)/shard_map/ppermute | solution.py:31
  376.7 7.7 %collective-permute-start.13 = (f32[16,128]{1,0:T(8,128)S(1)}, f32[16,128]{1,0:T(8,128)S(1)}, u32[]{:S(2)}, u32[]{:S(2)}) collective-permute-start(f32[16,128]{1,0:T(8,128)S(1)} %get-tuple-element.73), channel_id=1, source_target_pairs={{1,0},{2,1},{3,2},{4,3},{5,4},{6,5},{7,6},{8,7},{9,8},{10,9},{11,1... | collective-permute-start | bytes 24584 | tf_op jit(solution)/shard_map/ppermute | solution.py:33

commit v2 on v1

--- a/solution.py
+++ b/solution.py
@@ -37,34 +37,31 @@
     return cells
 
 
-def tap_places(offsets):
-    reach = offsets + W
-    return reach // DEC, reach % DEC
-
-
-def blur_down(wide, weights, offsets, rows_out):
-    shifts, phases = tap_places(offsets)
-    quads = wide.reshape(wide.shape[0] // DEC, DEC, wide.shape[1])
+def tap_table(weights, offsets):
+    reach = jnp.arange(2 * W + 1, dtype=jnp.int32)
+    hits = (offsets[None, :] + W) == reach[:, None]
+    return jnp.sum(jnp.where(hits, weights[None, :], jnp.float32(0.0)), axis=1)
+
+
+def blur_down(wide, table, rows_out):
+    quads = wide.reshape(wide.shape[0] // DEC, DEC, wide.shape[1]).astype(jnp.float32)
     total = jnp.zeros((rows_out, wide.shape[1]), jnp.float32)
-    for number in range(weights.shape[0]):
-        piece = lax.dynamic_slice(
-            quads, (shifts[number], phases[number], 0), (rows_out, 1, wide.shape[1])
-        )[:, 0, :]
-        total = total + weights[number] * piece.astype(jnp.float32)
+    for reach in range(2 * W + 1):
+        shift, phase = divmod(reach, DEC)
+        total = total + table[reach] * quads[shift : shift + rows_out, phase, :]
     return total
 
 
-def blur_up(coarse_wide, weights, offsets, margin):
-    shifts, phases = tap_places(offsets)
+def blur_up(coarse_wide, table, margin):
     rows = coarse_wide.shape[0] - 2 * margin
-    columns = coarse_wide.shape[1]
-    parts = [jnp.zeros((rows, columns), jnp.float32) for _ in range(DEC)]
-    for number in range(weights.shape[0]):
-        piece = lax.dynamic_slice_in_dim(coarse_wide, margin + 2 - shifts[number], rows, 0)
-        for phase in range(DEC):
-            scale = jnp.where(phases[number] == phase, weights[number], jnp.float32(0.0))
-            parts[phase] = parts[phase] + scale * piece
-    return jnp.stack(parts, axis=1).reshape(rows * DEC, columns)
+    parts = []
+    for phase in range(DEC):
+        part = jnp.zeros((rows, coarse_wide.shape[1]), jnp.float32)
+        for shift in range((2 * W - phase) // DEC + 1):
+            start = margin + 2 - shift
+            part = part + table[DEC * shift + phase] * coarse_wide[start : start + rows]
+        parts.append(part)
+    return jnp.stack(parts, axis=1).reshape(rows * DEC, coarse_wide.shape[1])
 
 
 def total_kernel(rows, cols, part_ref, out_ref, col_held, row_held, sends, receipts):
@@ -196,9 +193,10 @@
     multispectral, hyperspectral, row_start, col_factor, band_factor, response, blur_taps, offsets
 ):
     low_reach = (W + DEC - 1) // DEC
+    table = tap_table(blur_taps, offsets)
     columns = lax.all_gather(col_factor, "row", axis=1, tiled=True)
     column_wide = extended(columns, (("col", 0),), W)
-    coarse_columns = blur_down(column_wide, blur_taps, offsets, columns.shape[0] // DEC)
+    coarse_columns = blur_down(column_wide, table, columns.shape[0] // DEC)
     merged = jnp.dot(response, band_factor, precision=FULL_PRECISION)
     multi_pairs = (merged[:, None, :] * columns.astype(jnp.float32)[None, :, :]).astype(
         jnp.bfloat16
@@ -237,8 +235,8 @@
 
     def operate(values):
         fine_wide = extended(values, ((grid, 0),), fine_reach)
-        coarse_wide = blur_down(fine_wide, blur_taps, offsets, coarse_rows + 2 * low_reach)
-        restored = blur_up(coarse_wide, blur_taps, offsets, low_reach)
+        coarse_wide = blur_down(fine_wide, table, coarse_rows + 2 * low_reach)
+        restored = blur_up(coarse_wide, table, low_reach)
         return (
             jnp.dot(restored, hyper_gram, precision=FULL_PRECISION)
             + jnp.dot(values, multi_gram, precision=FULL_PRECISION)
@@ -246,7 +244,7 @@
         )
 
     hyper_wide = extended(hyper_sums, ((grid, 0),), low_reach)
-    right_side = blur_up(hyper_wide, blur_taps, offsets, low_reach) + multi_sums
+    right_side = blur_up(hyper_wide, table, low_reach) + multi_sums
     solution = start_rows
     residual = right_side - operate(solution)
     direction = residual

time: 431 us -> 424 us (0.984)
  between operations: 113 us -> 10.9 us
  other arithmetic: 43.8 us -> 136 us
  Pallas kernels: 145 us -> 154 us
    another operation x26 -> x19, other arithmetic: 1.58 us -> 63.6 us  [blur_up(): return jnp.stack(parts, axis=1).reshape(rows * DEC, coarse_wide.shape[1])]
    add x10 -> x7, other arithmetic: 34.3 us -> 64.8 us  [the longest x6 64.2 us: blur_down(): total = total + table[reach] * quads[shift:shift + rows_out, phase, :]]
    pallas_call x1, Pallas kernels: 30.3 us -> 39.6 us  [col_scatter(): pl.pallas_call(functools.partial(scatter_kernel, cols), out_shape=(jax.Sh...]
    ppermute x7, starting transfers between devices: 43.3 us -> 37 us  [extended(): lax.ppermute(head, axis, [((i + 1) % count, i) for i in range(count)])]
  transfers between devices with their start and end apart: 14 -> 14, of which waited for: 4 -> 5; matrix products, arithmetic and copies ran while one was open for 7% -> 10% of each run, Pallas kernels for 7% -> 9%
where the time goes in v2:
time: 424 us; the launch traced here: 420 us
  Pallas kernels  154 us (36%)
  other arithmetic  136 us (32%)
  starting transfers between devices  43.4 us (10%)
  local copies, waits for them, and re-layouts  24.3 us (6%)
  blocking collectives  22.5 us (5%)
  matrix products  20.5 us (5%)
  between operations  10.9 us (3%)
  waiting for transfers between devices  8.85 us (2%)
    pallas_call x8, Pallas kernels, grid_totals(): pl.pallas_call(functools.partial(total_kernel, rows, cols), out_shape=jax...  114 us
    add x6, other arithmetic, blur_down(): total = total + table[reach] * quads[shift:shift + rows_out, phase, :]  64.2 us
    another operation x19, other arithmetic, blur_up(): return jnp.stack(parts, axis=1).reshape(rows * DEC, coarse_wide.shape[1])  63.6 us
    pallas_call x1, Pallas kernels, col_scatter(): pl.pallas_call(functools.partial(scatter_kernel, cols), out_shape=(jax.Sh...  39.6 us
    ppermute x7, starting transfers between devices, extended(): lax.ppermute(head, axis, [((i + 1) % count, i) for i in range(count)])  37 us
    all_gather x1, blocking collectives, body(): columns = lax.all_gather(col_factor, 'row', axis=1, tiled=True)  22.5 us
    ppermute x7, waiting for transfers between devices, extended(): lax.ppermute(tail, axis, [(i, (i + 1) % count) for i in range(count)])  8.69 us
    slice x7, local copies, waits for them, and re-layouts, grid_totals(): return [summed[0, number] for number in range(len(parts))]  8.59 us
  transfers between devices with their start and end apart: 14, of which 5 were waited for; matrix products, arithmetic and copies ran while one was open for 10% of the time, Pallas kernels for 9%

profile of v2, /device:TPU:0, one launch (start us, length us, event | category | flops | bytes accessed | tf_op | source)
XLA Modules:
  0.0 420.3 jit_solution(9696895349349495921)
XLA Ops:
  2.9 6.6 %collective-permute-start.5 = (f32[16,128]{1,0:T(8,128)S(1)}, f32[16,128]{1,0:T(8,128)S(1)}, u32[]{:S(2)}, u32[]{:S(2)}) collective-permute-start(f32[16,128]{1,0:T(8,128)S(1)} %get-tuple-element.134), channel_id=1, source_target_pairs={{1,0},{2,1},{3,2},{4,3},{5,4},{6,5},{7,6},{8,7},{9,8},{10,9},{11,1... | collective-permute-start | bytes 24584 | tf_op jit(solution)/shard_map/ppermute | solution.py:33
  9.6 22.5 %all_gather.3 = bf16[512,128]{0,1:T(8,128)(2,1)S(1)} all-gather(bf16[512,8]{0,1:T(8,128)(2,1)} %param.11), channel_id=1, replica_groups=mesh['row'=16,'col'=8] {'row'}, dimensions={1}, use_global_device_ids=true | all-gather | bytes 139264 | tf_op jit(solution)/shard_map/all_gather | solution.py:197
  44.5 10.6 %bitcast_add_fusion = (f32[128,128]{1,0:T(8,128)S(1)}, f32[128,1,128]{2,0,1:T(8,128)S(1)}) fusion(f32[128,1,128]{2,0,1:T(8,128)S(1)} %bitcast.214, f32[]{:T(128)} %bitcast.22, f32[128,1,128]{2,0,1:T(8,128)S(1)} %bitcast.237, f32[]{:T(128)} %bitcast.20, f32[128,1,128]{2,0,1:T(8,128)S(1)} %bitcast.236, f32[]{:T(128)} %bitcast.19, ...), kind=kLoop, calls=%fused_computation.56 | loop fusion | flops 540672 | bytes 1245252 | tf_op jit(solution)/shard_map/add | solution.py:51
  56.2 7.5 %fusion.3 = f32[512,128]{0,1:T(8,128)S(1)} fusion(bf16[96,512,128]{2,1,0:T(8,128)(2,1)} %param.9, f32[128,128]{0,1:T(8,128)S(1)} %copy.396, f32[96,128]{1,0:T(8,128)S(1)} %copy-done.2), kind=kOutput, calls=%fused_computation.6 | convolution fusion | flops 1613758464 | bytes 12959744 | tf_op jit(solution)/shard_map/kij,kjr->ir/dot_general | solution.py:208
  65.6 39.6 %shard_map.95 = (f32[320,128]{1,0:T(8,128)}, f32[256,128]{1,0:T(8,128)}) custom-call(f32[8,320,128]{2,1,0:T(8,128)} %pad_maximum_fusion.blocks_ref, f32[256,128]{1,0:T(8,128)} %pad_maximum_fusion.7.gram_ref), custom_call_target="tpu_custom_call" | custom-call | tf_op jit(solution)/shard_map/pallas_call | solution.py:174
  125.5 10.7 %fusion.90 = f32[68,128]{1,0:T(8,128)S(1)} fusion(f32[68,1,128]{2,1,0:T(1,128)S(1)} %get-tuple-element.105, f32[68,1,128]{2,1,0:T(1,128)S(1)} %get-tuple-element.90, f32[68,1,128]{2,1,0:T(1,128)S(1)} %get-tuple-element.91, f32[68,1,128]{2,1,0:T(1,128)S(1)} %get-tuple-element.92, f32[68,1,128]{2,1,0:T(1,128)S(1)} %get-tuple-element.93, ...), kind=kLoop, calls=%fused_computation.206 | loop fusion | flops 287232 | bytes 626756 | tf_op jit(solution)/shard_map/add | solution.py:51
  141.3 5.6 %fusion.118 = (f32[64,1,128]{2,0,1:T(8,128)S(1)}, f32[64,1,128]{2,0,1:T(8,128)S(1)}) fusion(f32[68,128]{1,0:T(8,128)S(1)} %fusion.90, f32[]{:T(128)} %bitcast.22, f32[]{:T(128)} %bitcast.17, f32[]{:T(128)} %bitcast.13, f32[]{:T(128)} %bitcast.9, f32[]{:T(128)} %bitcast, f32[]{:T(128)} %bitcast.18, f32[]{:T(128)} %bitcast.14, f32[]{:T(128)} %bitcast.10, ...), kind=kLoop, calls=%fused_computation.255 | loop fusion | flops 131072 | bytes 229412 | tf_op jit(solution)/shard_map/stack | solution.py:64
  147.6 7.2 %collective-permute-start.7 = (f32[16,128]{1,0:T(8,128)S(1)}, f32[16,128]{1,0:T(8,128)S(1)}, u32[]{:S(2)}, u32[]{:S(2)}) collective-permute-start(f32[16,128]{1,0:T(8,128)S(1)} %get-tuple-element.130), channel_id=1, source_target_pairs={{1,0},{2,1},{3,2},{4,3},{5,4},{6,5},{7,6},{8,7},{9,8},{10,9},{11,1... | collective-permute-start | bytes 24584 | tf_op jit(solution)/shard_map/ppermute | solution.py:33
  156.5 10.7 %fusion.72 = f32[68,128]{1,0:T(8,128)S(1)} fusion(f32[68,1,128]{2,1,0:T(1,128)S(1)} %get-tuple-element.88, f32[68,1,128]{2,1,0:T(1,128)S(1)} %get-tuple-element.73, f32[68,1,128]{2,1,0:T(1,128)S(1)} %get-tuple-element.74, f32[68,1,128]{2,1,0:T(1,128)S(1)} %get-tuple-element.75, f32[68,1,128]{2,1,0:T(1,128)S(1)} %get-tuple-element.76, ...), kind=kLoop, calls=%fused_computation.171 | loop fusion | flops 287232 | bytes 626756 | tf_op jit(solution)/shard_map/add | solution.py:51
  172.2 5.6 %fusion.116 = (f32[64,1,128]{2,0,1:T(8,128)S(1)}, f32[64,1,128]{2,0,1:T(8,128)S(1)}) fusion(f32[68,128]{1,0:T(8,128)S(1)} %fusion.72, f32[]{:T(128)} %bitcast.22, f32[]{:T(128)} %bitcast.17, f32[]{:T(128)} %bitcast.13, f32[]{:T(128)} %bitcast.9, f32[]{:T(128)} %bitcast, f32[]{:T(128)} %bitcast.18, f32[]{:T(128)} %bitcast.14, f32[]{:T(128)} %bitcast.10, ...), kind=kLoop, calls=%fused_computation.252 | loop fusion | flops 131072 | bytes 229412 | tf_op jit(solution)/shard_map/stack | solution.py:64
  181.0 15.1 %shard_map.96 = f32[8,128]{1,0:T(8,128)} custom-call(f32[8,128]{1,0:T(8,128)} %broadcast_in_dim.30.part_ref), custom_call_target="tpu_custom_call" | custom-call | tf_op jit(solution)/shard_map/pallas_call | solution.py:120
  200.6 13.5 %shard_map.97 = f32[8,128]{1,0:T(8,128)} custom-call(f32[8,128]{1,0:T(8,128)} %broadcast_in_dim.31.part_ref), custom_call_target="tpu_custom_call" | custom-call | tf_op jit(solution)/shard_map/pallas_call | solution.py:120
  217.6 6.4 %collective-permute-start.9 = (f32[16,128]{1,0:T(8,128)S(1)}, f32[16,128]{1,0:T(8,128)S(1)}, u32[]{:S(2)}, u32[]{:S(2)}) collective-permute-start(f32[16,128]{1,0:T(8,128)S(1)} %get-tuple-element.128), channel_id=1, source_target_pairs={{1,0},{2,1},{3,2},{4,3},{5,4},{6,5},{7,6},{8,7},{9,8},{10,9},{11,1... | collective-permute-start | bytes 24584 | tf_op jit(solution)/shard_map/ppermute | solution.py:33
  225.7 10.7 %fusion.54 = f32[68,128]{1,0:T(8,128)S(1)} fusion(f32[68,1,128]{2,1,0:T(1,128)S(1)} %get-tuple-element.71, f32[68,1,128]{2,1,0:T(1,128)S(1)} %get-tuple-element.56, f32[68,1,128]{2,1,0:T(1,128)S(1)} %get-tuple-element.57, f32[68,1,128]{2,1,0:T(1,128)S(1)} %get-tuple-element.58, f32[68,1,128]{2,1,0:T(1,128)S(1)} %get-tuple-element.59, ...), kind=kLoop, calls=%fused_computation.136 | loop fusion | flops 287232 | bytes 626756 | tf_op jit(solution)/shard_map/add | solution.py:51
  249.5 15.1 %shard_map.98 = f32[8,128]{1,0:T(8,128)} custom-call(f32[8,128]{1,0:T(8,128)} %broadcast_in_dim.32.part_ref), custom_call_target="tpu_custom_call" | custom-call | tf_op jit(solution)/shard_map/pallas_call | solution.py:120
  269.0 13.5 %shard_map.99 = f32[8,128]{1,0:T(8,128)} custom-call(f32[8,128]{1,0:T(8,128)} %broadcast_in_dim.33.part_ref), custom_call_target="tpu_custom_call" | custom-call | tf_op jit(solution)/shard_map/pallas_call | solution.py:120
  286.0 6.4 %collective-permute-start.11 = (f32[16,128]{1,0:T(8,128)S(1)}, f32[16,128]{1,0:T(8,128)S(1)}, u32[]{:S(2)}, u32[]{:S(2)}) collective-permute-start(f32[16,128]{1,0:T(8,128)S(1)} %get-tuple-element.126), channel_id=1, source_target_pairs={{1,0},{2,1},{3,2},{4,3},{5,4},{6,5},{7,6},{8,7},{9,8},{10,9},{11,1... | collective-permute-start | bytes 24584 | tf_op jit(solution)/shard_map/ppermute | solution.py:33
  294.1 10.7 %fusion.36 = f32[68,128]{1,0:T(8,128)S(1)} fusion(f32[68,1,128]{2,1,0:T(1,128)S(1)} %get-tuple-element.54, f32[68,1,128]{2,1,0:T(1,128)S(1)} %get-tuple-element.39, f32[68,1,128]{2,1,0:T(1,128)S(1)} %get-tuple-element.40, f32[68,1,128]{2,1,0:T(1,128)S(1)} %get-tuple-element.41, f32[68,1,128]{2,1,0:T(1,128)S(1)} %get-tuple-element.42, ...), kind=kLoop, calls=%fused_computation.101 | loop fusion | flops 287232 | bytes 626756 | tf_op jit(solution)/shard_map/add | solution.py:51
  317.9 15.1 %shard_map.100 = f32[8,128]{1,0:T(8,128)} custom-call(f32[8,128]{1,0:T(8,128)} %broadcast_in_dim.34.part_ref), custom_call_target="tpu_custom_call" | custom-call | tf_op jit(solution)/shard_map/pallas_call | solution.py:120
  337.4 13.5 %shard_map.101 = f32[8,128]{1,0:T(8,128)} custom-call(f32[8,128]{1,0:T(8,128)} %broadcast_in_dim.35.part_ref), custom_call_target="tpu_custom_call" | custom-call | tf_op jit(solution)/shard_map/pallas_call | solution.py:120
  354.5 6.4 %collective-permute-start.13 = (f32[16,128]{1,0:T(8,128)S(1)}, f32[16,128]{1,0:T(8,128)S(1)}, u32[]{:S(2)}, u32[]{:S(2)}) collective-permute-start(f32[16,128]{1,0:T(8,128)S(1)} %get-tuple-element.124), channel_id=1, source_target_pairs={{1,0},{2,1},{3,2},{4,3},{5,4},{6,5},{7,6},{8,7},{9,8},{10,9},{11,1... | collective-permute-start | bytes 24584 | tf_op jit(solution)/shard_map/ppermute | solution.py:33
  362.6 10.7 %fusion.18 = f32[68,128]{1,0:T(8,128)S(1)} fusion(f32[68,1,128]{2,1,0:T(1,128)S(1)} %get-tuple-element.37, f32[68,1,128]{2,1,0:T(1,128)S(1)} %get-tuple-element.22, f32[68,1,128]{2,1,0:T(1,128)S(1)} %get-tuple-element.23, f32[68,1,128]{2,1,0:T(1,128)S(1)} %get-tuple-element.24, f32[68,1,128]{2,1,0:T(1,128)S(1)} %get-tuple-element.25, ...), kind=kLoop, calls=%fused_computation.66 | loop fusion | flops 287232 | bytes 626756 | tf_op jit(solution)/shard_map/add | solution.py:51
  386.4 15.1 %shard_map.102 = f32[8,128]{1,0:T(8,128)} custom-call(f32[8,128]{1,0:T(8,128)} %broadcast_in_dim.36.part_ref), custom_call_target="tpu_custom_call" | custom-call | tf_op jit(solution)/shard_map/pallas_call | solution.py:120
  406.7 13.5 %shard_map.103 = f32[8,128]{1,0:T(8,128)} custom-call(f32[8,128]{1,0:T(8,128)} %broadcast_in_dim.37.part_ref), custom_call_target="tpu_custom_call" | custom-call | tf_op jit(solution)/shard_map/pallas_call | solution.py:120
  (130 shorter events, 117.2 us)
Async XLA Ops:
  0.6 37.4 %copy-start = (f32[2,96]{1,0:T(2,128)S(1)}, f32[2,96]{1,0:T(2,128)}, u32[]{:S(2)}) copy-start(f32[2,96]{1,0:T(2,128)} %param.13) | copy-start | bytes 2308
  1.4 123.8 %collective-permute-start.4 = (f32[16,128]{1,0:T(8,128)S(1)}, f32[16,128]{1,0:T(8,128)S(1)}, u32[]{:S(2)}, u32[]{:S(2)}) collective-permute-start(f32[16,128]{1,0:T(8,128)S(1)} %get-tuple-element.133), channel_id=1, source_target_pairs={{0,1},{1,2},{2,3},{3,4},{4,5},{5,6},{6,7},{7,8},{8,9},{9,10},{10,1... | collective-permute-start | bytes 24584 | tf_op jit(solution)/shard_map/ppermute | solution.py:31
  2.9 122.2 %collective-permute-start.5 = (f32[16,128]{1,0:T(8,128)S(1)}, f32[16,128]{1,0:T(8,128)S(1)}, u32[]{:S(2)}, u32[]{:S(2)}) collective-permute-start(f32[16,128]{1,0:T(8,128)S(1)} %get-tuple-element.134), channel_id=1, source_target_pairs={{1,0},{2,1},{3,2},{4,3},{5,4},{6,5},{7,6},{8,7},{9,8},{10,9},{11,1... | collective-permute-start | bytes 24584 | tf_op jit(solution)/shard_map/ppermute | solution.py:33
  32.2 11.5 %collective-permute-start = (bf16[8,128]{1,0:T(8,128)(2,1)S(1)}, bf16[8,128]{1,0:T(8,128)(2,1)S(1)}, u32[]{:S(2)}, u32[]{:S(2)}) collective-permute-start(bf16[8,128]{1,0:T(8,128)(2,1)S(1)} %get-tuple-element.131), channel_id=1, source_target_pairs={{0,1},{1,2},{2,3},{3,4},{4,5},{5,6},{6,7},{7,0},{8,9},{9,10},{10,1... | collective-permute-start | bytes 6152 | tf_op jit(solution)/shard_map/ppermute | solution.py:31
  32.2 11.5 %collective-permute-start.1 = (bf16[8,128]{1,0:T(8,128)(2,1)S(1)}, bf16[8,128]{1,0:T(8,128)(2,1)S(1)}, u32[]{:S(2)}, u32[]{:S(2)}) collective-permute-start(bf16[8,128]{1,0:T(8,128)(2,1)S(1)} %get-tuple-element.132), channel_id=1, source_target_pairs={{1,0},{2,1},{3,2},{4,3},{5,4},{6,5},{7,6},{0,7},{9,8},{10,9},{11,1... | collective-permute-start | bytes 6152 | tf_op jit(solution)/shard_map/ppermute | solution.py:33
  42.6 13.5 %copy-start.2 = (f32[96,128]{1,0:T(8,128)S(1)}, f32[96,128]{1,0:T(8,128)}, u32[]{:S(2)}) copy-start(f32[96,128]{1,0:T(8,128)} %param.12) | copy-start | bytes 147460
  63.7 61.5 %copy-start.1 = (f32[256,128]{1,0:T(8,128)S(1)}, f32[256,128]{1,0:T(8,128)}, u32[]{:S(2)}) copy-start(f32[256,128]{1,0:T(8,128)} %param.10) | copy-start | bytes 393220
  105.3 42.0 %copy-start.3 = (f32[320,128]{1,0:T(8,128)S(1)}, f32[320,128]{1,0:T(8,128)}, u32[]{:S(2)}) copy-start(f32[320,128]{1,0:T(8,128)} %get-tuple-element.4) | copy-start | bytes 491524
  106.0 5.1 %collective-permute-start.2 = (f32[2,128]{1,0:T(2,128)S(1)}, f32[2,128]{1,0:T(2,128)S(1)}, u32[]{:S(2)}, u32[]{:S(2)}) collective-permute-start(f32[2,128]{1,0:T(2,128)S(1)} %get-tuple-element.19), channel_id=1, source_target_pairs={{1,0},{2,1},{3,2},{4,3},{5,4},{6,5},{7,6},{8,7},{9,8},{10,9},{11,1... | collective-permute-start | bytes 3080 | tf_op jit(solution)/shard_map/ppermute | solution.py:33
  106.0 8.4 %collective-permute-start.3 = (f32[2,128]{1,0:T(2,128)S(1)}, f32[2,128]{1,0:T(2,128)S(1)}, u32[]{:S(2)}, u32[]{:S(2)}) collective-permute-start(f32[2,128]{1,0:T(2,128)S(1)} %get-tuple-element.20), channel_id=1, source_target_pairs={{0,1},{1,2},{2,3},{3,4},{4,5},{5,6},{6,7},{7,8},{8,9},{9,10},{10,1... | collective-permute-start | bytes 3080 | tf_op jit(solution)/shard_map/ppermute | solution.py:31
  147.5 8.6 %collective-permute-start.6 = (f32[16,128]{1,0:T(8,128)S(1)}, f32[16,128]{1,0:T(8,128)S(1)}, u32[]{:S(2)}, u32[]{:S(2)}) collective-permute-start(f32[16,128]{1,0:T(8,128)S(1)} %get-tuple-element.129), channel_id=1, source_target_pairs={{0,1},{1,2},{2,3},{3,4},{4,5},{5,6},{6,7},{7,8},{8,9},{9,10},{10,1... | collective-permute-start | bytes 24584 | tf_op jit(solution)/shard_map/ppermute | solution.py:31
  147.6 8.5 %collective-permute-start.7 = (f32[16,128]{1,0:T(8,128)S(1)}, f32[16,128]{1,0:T(8,128)S(1)}, u32[]{:S(2)}, u32[]{:S(2)}) collective-permute-start(f32[16,128]{1,0:T(8,128)S(1)} %get-tuple-element.130), channel_id=1, source_target_pairs={{1,0},{2,1},{3,2},{4,3},{5,4},{6,5},{7,6},{8,7},{9,8},{10,9},{11,1... | collective-permute-start | bytes 24584 | tf_op jit(solution)/shard_map/ppermute | solution.py:33
  216.7 8.6 %collective-permute-start.8 = (f32[16,128]{1,0:T(8,128)S(1)}, f32[16,128]{1,0:T(8,128)S(1)}, u32[]{:S(2)}, u32[]{:S(2)}) collective-permute-start(f32[16,128]{1,0:T(8,128)S(1)} %get-tuple-element.127), channel_id=1, source_target_pairs={{0,1},{1,2},{2,3},{3,4},{4,5},{5,6},{6,7},{7,8},{8,9},{9,10},{10,1... | collective-permute-start | bytes 24584 | tf_op jit(solution)/shard_map/ppermute | solution.py:31
  217.6 7.7 %collective-permute-start.9 = (f32[16,128]{1,0:T(8,128)S(1)}, f32[16,128]{1,0:T(8,128)S(1)}, u32[]{:S(2)}, u32[]{:S(2)}) collective-permute-start(f32[16,128]{1,0:T(8,128)S(1)} %get-tuple-element.128), channel_id=1, source_target_pairs={{1,0},{2,1},{3,2},{4,3},{5,4},{6,5},{7,6},{8,7},{9,8},{10,9},{11,1... | collective-permute-start | bytes 24584 | tf_op jit(solution)/shard_map/ppermute | solution.py:33
  285.1 8.6 %collective-permute-start.10 = (f32[16,128]{1,0:T(8,128)S(1)}, f32[16,128]{1,0:T(8,128)S(1)}, u32[]{:S(2)}, u32[]{:S(2)}) collective-permute-start(f32[16,128]{1,0:T(8,128)S(1)} %get-tuple-element.125), channel_id=1, source_target_pairs={{0,1},{1,2},{2,3},{3,4},{4,5},{5,6},{6,7},{7,8},{8,9},{9,10},{10,1... | collective-permute-start | bytes 24584 | tf_op jit(solution)/shard_map/ppermute | solution.py:31
  286.0 7.7 %collective-permute-start.11 = (f32[16,128]{1,0:T(8,128)S(1)}, f32[16,128]{1,0:T(8,128)S(1)}, u32[]{:S(2)}, u32[]{:S(2)}) collective-permute-start(f32[16,128]{1,0:T(8,128)S(1)} %get-tuple-element.126), channel_id=1, source_target_pairs={{1,0},{2,1},{3,2},{4,3},{5,4},{6,5},{7,6},{8,7},{9,8},{10,9},{11,1... | collective-permute-start | bytes 24584 | tf_op jit(solution)/shard_map/ppermute | solution.py:33
  353.6 8.6 %collective-permute-start.12 = (f32[16,128]{1,0:T(8,128)S(1)}, f32[16,128]{1,0:T(8,128)S(1)}, u32[]{:S(2)}, u32[]{:S(2)}) collective-permute-start(f32[16,128]{1,0:T(8,128)S(1)} %get-tuple-element.123), channel_id=1, source_target_pairs={{0,1},{1,2},{2,3},{3,4},{4,5},{5,6},{6,7},{7,8},{8,9},{9,10},{10,1... | collective-permute-start | bytes 24584 | tf_op jit(solution)/shard_map/ppermute | solution.py:31
  354.5 7.7 %collective-permute-start.13 = (f32[16,128]{1,0:T(8,128)S(1)}, f32[16,128]{1,0:T(8,128)S(1)}, u32[]{:S(2)}, u32[]{:S(2)}) collective-permute-start(f32[16,128]{1,0:T(8,128)S(1)} %get-tuple-element.124), channel_id=1, source_target_pairs={{1,0},{2,1},{3,2},{4,3},{5,4},{6,5},{7,6},{8,7},{9,8},{10,9},{11,1... | collective-permute-start | bytes 24584 | tf_op jit(solution)/shard_map/ppermute | solution.py:33

commit v3 on v2

--- a/solution.py
+++ b/solution.py
@@ -37,31 +37,23 @@
     return cells
 
 
-def tap_table(weights, offsets):
-    reach = jnp.arange(2 * W + 1, dtype=jnp.int32)
-    hits = (offsets[None, :] + W) == reach[:, None]
-    return jnp.sum(jnp.where(hits, weights[None, :], jnp.float32(0.0)), axis=1)
-
-
-def blur_down(wide, table, rows_out):
-    quads = wide.reshape(wide.shape[0] // DEC, DEC, wide.shape[1]).astype(jnp.float32)
-    total = jnp.zeros((rows_out, wide.shape[1]), jnp.float32)
-    for reach in range(2 * W + 1):
-        shift, phase = divmod(reach, DEC)
-        total = total + table[reach] * quads[shift : shift + rows_out, phase, :]
-    return total
-
-
-def blur_up(coarse_wide, table, margin):
-    rows = coarse_wide.shape[0] - 2 * margin
-    parts = []
-    for phase in range(DEC):
-        part = jnp.zeros((rows, coarse_wide.shape[1]), jnp.float32)
-        for shift in range((2 * W - phase) // DEC + 1):
-            start = margin + 2 - shift
-            part = part + table[DEC * shift + phase] * coarse_wide[start : start + rows]
-        parts.append(part)
-    return jnp.stack(parts, axis=1).reshape(rows * DEC, coarse_wide.shape[1])
+def down_matrix(weights, offsets, rows_out, rows_in):
+    outer = lax.broadcasted_iota(jnp.int32, (rows_out, rows_in, 1), 0)
+    inner = lax.broadcasted_iota(jnp.int32, (rows_out, rows_in, 1), 1)
+    hits = inner == DEC * outer + offsets[None, None, :] + W
+    return jnp.sum(jnp.where(hits, weights[None, None, :], jnp.float32(0.0)), axis=2)
+
+
+def up_matrix(weights, offsets, rows_in, low_margin):
+    rows_out = (rows_in - 2 * low_margin) * DEC
+    outer = lax.broadcasted_iota(jnp.int32, (rows_out, rows_in, 1), 0)
+    inner = lax.broadcasted_iota(jnp.int32, (rows_out, rows_in, 1), 1)
+    hits = DEC * inner == outer + DEC * low_margin - offsets[None, None, :]
+    return jnp.sum(jnp.where(hits, weights[None, None, :], jnp.float32(0.0)), axis=2)
+
+
+def apply_band(matrix, values):
+    return jnp.dot(matrix, values.astype(jnp.float32), precision=FULL_PRECISION)
 
 
 def total_kernel(rows, cols, part_ref, out_ref, col_held, row_held, sends, receipts):
@@ -193,10 +185,10 @@
     multispectral, hyperspectral, row_start, col_factor, band_factor, response, blur_taps, offsets
 ):
     low_reach = (W + DEC - 1) // DEC
-    table = tap_table(blur_taps, offsets)
     columns = lax.all_gather(col_factor, "row", axis=1, tiled=True)
     column_wide = extended(columns, (("col", 0),), W)
-    coarse_columns = blur_down(column_wide, table, columns.shape[0] // DEC)
+    column_down = down_matrix(blur_taps, offsets, columns.shape[0] // DEC, column_wide.shape[0])
+    coarse_columns = apply_band(column_down, column_wide)
     merged = jnp.dot(response, band_factor, precision=FULL_PRECISION)
     multi_pairs = (merged[:, None, :] * columns.astype(jnp.float32)[None, :, :]).astype(
         jnp.bfloat16
@@ -233,10 +225,13 @@
     coarse_rows = fine_rows // DEC
     fine_reach = W + DEC * low_reach
 
+    lifting = up_matrix(blur_taps, offsets, coarse_rows + 2 * low_reach, low_reach)
+    lowering = down_matrix(blur_taps, offsets, coarse_rows + 2 * low_reach, fine_rows + 2 * fine_reach)
+    blurring = jnp.dot(lifting, lowering, precision=FULL_PRECISION)
+
     def operate(values):
         fine_wide = extended(values, ((grid, 0),), fine_reach)
-        coarse_wide = blur_down(fine_wide, table, coarse_rows + 2 * low_reach)
-        restored = blur_up(coarse_wide, table, low_reach)
+        restored = apply_band(blurring, fine_wide)
         return (
             jnp.dot(restored, hyper_gram, precision=FULL_PRECISION)
             + jnp.dot(values, multi_gram, precision=FULL_PRECISION)
@@ -244,7 +239,7 @@
         )
 
     hyper_wide = extended(hyper_sums, ((grid, 0),), low_reach)
-    right_side = blur_up(hyper_wide, table, low_reach) + multi_sums
+    right_side = apply_band(lifting, hyper_wide) + multi_sums
     solution = start_rows
     residual = right_side - operate(solution)
     direction = residual

time: 424 us -> 293 us (0.69)
  other arithmetic: 136 us -> 8.86 us
  Pallas kernels: 154 us -> 145 us
  matrix products: 20.5 us -> 26.3 us
  starting transfers between devices: 43.4 us -> 47.7 us
    add x7 -> x1, other arithmetic: 64.8 us -> 0.01 us  [up_matrix(): hits = DEC * inner == outer + DEC * low_margin - offsets[None, None, :]]
    another operation x19 -> x0, other arithmetic: 63.6 us -> none  [blur_up(): return jnp.stack(parts, axis=1).reshape(rows * DEC, coarse_wide.shape[1])]
    pallas_call x1, Pallas kernels: 39.6 us -> 30.3 us  [col_scatter(): pl.pallas_call(functools.partial(scatter_kernel, cols), out_shape=(jax.Sh...]
    dot_general x0 -> x8, matrix products: none -> 6.42 us  [the longest x7 5.94 us: apply_band(): return jnp.dot(matrix, values.astype(jnp.float32), precision=FULL_PRECISION)]
    ppermute x7, starting transfers between devices: 37 us -> 43.3 us  [extended(): lax.ppermute(head, axis, [((i + 1) % count, i) for i in range(count)])]
  transfers between devices with their start and end apart: 14 -> 14, of which waited for: 5 -> 4; matrix products, arithmetic and copies ran while one was open for 10% -> 8% of each run, Pallas kernels for 9% -> 10%
where the time goes in v3:
time: 293 us; the launch traced here: 290 us
  Pallas kernels  145 us (49%)
  starting transfers between devices  47.7 us (16%)
  matrix products  26.3 us (9%)
  blocking collectives  25.9 us (9%)
  local copies, waits for them, and re-layouts  20.8 us (7%)
  between operations  10.6 us (4%)
  other arithmetic  8.86 us (3%)
  waiting for transfers between devices  5.48 us (2%)
    pallas_call x8, Pallas kernels, grid_totals(): pl.pallas_call(functools.partial(total_kernel, rows, cols), out_shape=jax...  115 us
    ppermute x7, starting transfers between devices, extended(): lax.ppermute(head, axis, [((i + 1) % count, i) for i in range(count)])  43.3 us
    pallas_call x1, Pallas kernels, col_scatter(): pl.pallas_call(functools.partial(scatter_kernel, cols), out_shape=(jax.Sh...  30.3 us
    all_gather x1, blocking collectives, body(): columns = lax.all_gather(col_factor, 'row', axis=1, tiled=True)  25.9 us
    slice x7, local copies, waits for them, and re-layouts, grid_totals(): return [summed[0, number] for number in range(len(parts))]  8.6 us
    dot_general x1, matrix products, body(): jnp.einsum('kij,kjr->ir', hyperspectral, hyper_pairs, preferred_element_t...  7.48 us
    dot_general x7, matrix products, apply_band(): return jnp.dot(matrix, values.astype(jnp.float32), precision=FULL_PRECISION)  5.94 us
  transfers between devices with their start and end apart: 14, of which 4 were waited for; matrix products, arithmetic and copies ran while one was open for 8% of the time, Pallas kernels for 10%

profile of v3, /device:TPU:0, one launch (start us, length us, event | category | flops | bytes accessed | tf_op | source)
XLA Modules:
  0.0 290.4 jit_solution(16448232638544929)
XLA Ops:
  0.6 25.9 %all_gather.3 = bf16[512,128]{0,1:T(8,128)(2,1)S(1)} all-gather(bf16[512,8]{0,1:T(8,128)(2,1)} %param.11), channel_id=1, replica_groups=mesh['row'=16,'col'=8] {'row'}, dimensions={1}, use_global_device_ids=true | all-gather | bytes 139264 | tf_op jit(solution)/shard_map/all_gather | solution.py:188
  26.7 1.5 collective-permute-start
  28.2 2.6 collective-permute-start.1
  31.5 7.2 %collective-permute-start.5 = (f32[16,128]{1,0:T(8,128)S(1)}, f32[16,128]{1,0:T(8,128)S(1)}, u32[]{:S(2)}, u32[]{:S(2)}) collective-permute-start(f32[16,128]{1,0:T(8,128)S(1)} %get-tuple-element.27), channel_id=1, source_target_pairs={{1,0},{2,1},{3,2},{4,3},{5,4},{6,5},{7,6},{8,7},{9,8},{10,9},{11,1... | collective-permute-start | bytes 24584 | tf_op jit(solution)/shard_map/ppermute | solution.py:33
  42.2 3.7 %convolution_bitcast_fusion = f32[2048,128]{0,1:T(8,128)S(1)} fusion(bf16[2,2048,512]{2,1,0:T(8,128)(2,1)} %param.8, f32[512,128]{0,1:T(8,128)S(1)} %convert_element_type.20, f32[2,128]{1,0:T(2,128)S(1)} %fusion.70), kind=kOutput, calls=%fused_computation.4 | convolution fusion | flops 537133056 | bytes 5506048 | tf_op jit(solution)/shard_map/kij,kjr->ir/dot_general | solution.py:197
  47.7 7.5 %fusion.3 = f32[512,128]{0,1:T(8,128)S(1)} fusion(bf16[96,512,128]{2,1,0:T(8,128)(2,1)} %param.9, f32[128,128]{0,1:T(8,128)S(1)} %copy.15, f32[96,128]{1,0:T(8,128)S(1)} %copy-done.2), kind=kOutput, calls=%fused_computation.8 | convolution fusion | flops 1613758464 | bytes 12959744 | tf_op jit(solution)/shard_map/kij,kjr->ir/dot_general | solution.py:200
  57.1 30.3 %shard_map.95 = (f32[320,128]{1,0:T(8,128)}, f32[256,128]{1,0:T(8,128)}) custom-call(f32[8,320,128]{2,1,0:T(8,128)} %pad_maximum_fusion.blocks_ref, f32[256,128]{1,0:T(8,128)} %pad_maximum_fusion.1.gram_ref), custom_call_target="tpu_custom_call" | custom-call | tf_op jit(solution)/shard_map/pallas_call | solution.py:166
  91.2 7.2 %collective-permute-start.3 = (f32[2,128]{1,0:T(2,128)S(1)}, f32[2,128]{1,0:T(2,128)S(1)}, u32[]{:S(2)}, u32[]{:S(2)}) collective-permute-start(f32[2,128]{1,0:T(2,128)S(1)} %get-tuple-element.15), channel_id=1, source_target_pairs={{1,0},{2,1},{3,2},{4,3},{5,4},{6,5},{7,6},{8,7},{9,8},{10,9},{11,1... | collective-permute-start | bytes 3080 | tf_op jit(solution)/shard_map/ppermute | solution.py:33
  101.2 7.2 %collective-permute-start.7 = (f32[16,128]{1,0:T(8,128)S(1)}, f32[16,128]{1,0:T(8,128)S(1)}, u32[]{:S(2)}, u32[]{:S(2)}) collective-permute-start(f32[16,128]{1,0:T(8,128)S(1)} %get-tuple-element.23), channel_id=1, source_target_pairs={{1,0},{2,1},{3,2},{4,3},{5,4},{6,5},{7,6},{8,7},{9,8},{10,9},{11,1... | collective-permute-start | bytes 24584 | tf_op jit(solution)/shard_map/ppermute | solution.py:33
  108.3 1.3 collective-permute-done.6
  111.7 1.4 fusion.54
  113.6 15.1 %shard_map.96 = f32[8,128]{1,0:T(8,128)} custom-call(f32[8,128]{1,0:T(8,128)} %broadcast_in_dim.58.part_ref), custom_call_target="tpu_custom_call" | custom-call | tf_op jit(solution)/shard_map/pallas_call | solution.py:112
  128.8 1.3 fusion.69
  133.3 13.5 %shard_map.97 = f32[8,128]{1,0:T(8,128)} custom-call(f32[8,128]{1,0:T(8,128)} %broadcast_in_dim.59.part_ref), custom_call_target="tpu_custom_call" | custom-call | tf_op jit(solution)/shard_map/pallas_call | solution.py:112
  150.5 6.4 %collective-permute-start.9 = (f32[16,128]{1,0:T(8,128)S(1)}, f32[16,128]{1,0:T(8,128)S(1)}, u32[]{:S(2)}, u32[]{:S(2)}) collective-permute-start(f32[16,128]{1,0:T(8,128)S(1)} %get-tuple-element.21), channel_id=1, source_target_pairs={{1,0},{2,1},{3,2},{4,3},{5,4},{6,5},{7,6},{8,7},{9,8},{10,9},{11,1... | collective-permute-start | bytes 24584 | tf_op jit(solution)/shard_map/ppermute | solution.py:33
  161.5 15.1 %shard_map.98 = f32[8,128]{1,0:T(8,128)} custom-call(f32[8,128]{1,0:T(8,128)} %broadcast_in_dim.60.part_ref), custom_call_target="tpu_custom_call" | custom-call | tf_op jit(solution)/shard_map/pallas_call | solution.py:112
  181.0 13.5 %shard_map.99 = f32[8,128]{1,0:T(8,128)} custom-call(f32[8,128]{1,0:T(8,128)} %broadcast_in_dim.61.part_ref), custom_call_target="tpu_custom_call" | custom-call | tf_op jit(solution)/shard_map/pallas_call | solution.py:112
  198.0 6.4 %collective-permute-start.11 = (f32[16,128]{1,0:T(8,128)S(1)}, f32[16,128]{1,0:T(8,128)S(1)}, u32[]{:S(2)}, u32[]{:S(2)}) collective-permute-start(f32[16,128]{1,0:T(8,128)S(1)} %get-tuple-element.19), channel_id=1, source_target_pairs={{1,0},{2,1},{3,2},{4,3},{5,4},{6,5},{7,6},{8,7},{9,8},{10,9},{11,1... | collective-permute-start | bytes 24584 | tf_op jit(solution)/shard_map/ppermute | solution.py:33
  208.9 15.1 %shard_map.100 = f32[8,128]{1,0:T(8,128)} custom-call(f32[8,128]{1,0:T(8,128)} %broadcast_in_dim.62.part_ref), custom_call_target="tpu_custom_call" | custom-call | tf_op jit(solution)/shard_map/pallas_call | solution.py:112
  228.5 13.5 %shard_map.101 = f32[8,128]{1,0:T(8,128)} custom-call(f32[8,128]{1,0:T(8,128)} %broadcast_in_dim.63.part_ref), custom_call_target="tpu_custom_call" | custom-call | tf_op jit(solution)/shard_map/pallas_call | solution.py:112
  245.5 6.4 %collective-permute-start.13 = (f32[16,128]{1,0:T(8,128)S(1)}, f32[16,128]{1,0:T(8,128)S(1)}, u32[]{:S(2)}, u32[]{:S(2)}) collective-permute-start(f32[16,128]{1,0:T(8,128)S(1)} %get-tuple-element.17), channel_id=1, source_target_pairs={{1,0},{2,1},{3,2},{4,3},{5,4},{6,5},{7,6},{8,7},{9,8},{10,9},{11,1... | collective-permute-start | bytes 24584 | tf_op jit(solution)/shard_map/ppermute | solution.py:33
  256.4 15.1 %shard_map.102 = f32[8,128]{1,0:T(8,128)} custom-call(f32[8,128]{1,0:T(8,128)} %broadcast_in_dim.64.part_ref), custom_call_target="tpu_custom_call" | custom-call | tf_op jit(solution)/shard_map/pallas_call | solution.py:112
  274.0 1.4 multiply_reduce_fusion
  276.8 13.5 %shard_map.103 = f32[8,128]{1,0:T(8,128)} custom-call(f32[8,128]{1,0:T(8,128)} %broadcast_in_dim.65.part_ref), custom_call_target="tpu_custom_call" | custom-call | tf_op jit(solution)/shard_map/pallas_call | solution.py:112
  (99 shorter events, 47.7 us)
Async XLA Ops:
  0.6 40.2 %copy-start = (f32[2,96]{1,0:T(2,128)S(1)}, f32[2,96]{1,0:T(2,128)}, u32[]{:S(2)}) copy-start(f32[2,96]{1,0:T(2,128)} %param.13) | copy-start | bytes 2308
  26.7 20.1 %collective-permute-start = (bf16[8,128]{0,1:T(8,128)(2,1)S(1)}, bf16[8,128]{0,1:T(8,128)(2,1)S(1)}, u32[]{:S(2)}, u32[]{:S(2)}) collective-permute-start(bf16[8,128]{0,1:T(8,128)(2,1)S(1)} %get-tuple-element.24), channel_id=1, source_target_pairs={{0,1},{1,2},{2,3},{3,4},{4,5},{5,6},{6,7},{7,0},{8,9},{9,10},{10,1... | collective-permute-start | bytes 6152 | tf_op jit(solution)/shard_map/ppermute | solution.py:31
  28.2 18.6 %collective-permute-start.1 = (bf16[8,128]{0,1:T(8,128)(2,1)S(1)}, bf16[8,128]{0,1:T(8,128)(2,1)S(1)}, u32[]{:S(2)}, u32[]{:S(2)}) collective-permute-start(bf16[8,128]{0,1:T(8,128)(2,1)S(1)} %get-tuple-element.25), channel_id=1, source_target_pairs={{1,0},{2,1},{3,2},{4,3},{5,4},{6,5},{7,6},{0,7},{9,8},{10,9},{11,1... | collective-permute-start | bytes 6152 | tf_op jit(solution)/shard_map/ppermute | solution.py:33
  31.5 66.8 %collective-permute-start.4 = (f32[16,128]{1,0:T(8,128)S(1)}, f32[16,128]{1,0:T(8,128)S(1)}, u32[]{:S(2)}, u32[]{:S(2)}) collective-permute-start(f32[16,128]{1,0:T(8,128)S(1)} %get-tuple-element.26), channel_id=1, source_target_pairs={{0,1},{1,2},{2,3},{3,4},{4,5},{5,6},{6,7},{7,8},{8,9},{9,10},{10,1... | collective-permute-start | bytes 24584 | tf_op jit(solution)/shard_map/ppermute | solution.py:31
  31.5 66.8 %collective-permute-start.5 = (f32[16,128]{1,0:T(8,128)S(1)}, f32[16,128]{1,0:T(8,128)S(1)}, u32[]{:S(2)}, u32[]{:S(2)}) collective-permute-start(f32[16,128]{1,0:T(8,128)S(1)} %get-tuple-element.27), channel_id=1, source_target_pairs={{1,0},{2,1},{3,2},{4,3},{5,4},{6,5},{7,6},{8,7},{9,8},{10,9},{11,1... | collective-permute-start | bytes 24584 | tf_op jit(solution)/shard_map/ppermute | solution.py:33
  38.9 7.0 %copy-start.3 = (f32[9]{0:T(128)S(1)}, f32[9]{0:T(128)}, u32[]{:S(2)}) copy-start(f32[9]{0:T(128)} %param.14) | copy-start | bytes 112
  38.9 7.0 %copy-start.4 = (s32[9]{0:T(128)S(1)}, s32[9]{0:T(128)}, u32[]{:S(2)}) copy-start(s32[9]{0:T(128)} %param.15) | copy-start | bytes 112
  42.2 5.5 %copy-start.2 = (f32[96,128]{1,0:T(8,128)S(1)}, f32[96,128]{1,0:T(8,128)}, u32[]{:S(2)}) copy-start(f32[96,128]{1,0:T(8,128)} %param.12) | copy-start | bytes 147460
  55.2 43.2 %copy-start.1 = (f32[256,128]{1,0:T(8,128)S(1)}, f32[256,128]{1,0:T(8,128)}, u32[]{:S(2)}) copy-start(f32[256,128]{1,0:T(8,128)} %param.10) | copy-start | bytes 393220
  91.2 8.6 %collective-permute-start.2 = (f32[2,128]{1,0:T(2,128)S(1)}, f32[2,128]{1,0:T(2,128)S(1)}, u32[]{:S(2)}, u32[]{:S(2)}) collective-permute-start(f32[2,128]{1,0:T(2,128)S(1)} %get-tuple-element.14), channel_id=1, source_target_pairs={{0,1},{1,2},{2,3},{3,4},{4,5},{5,6},{6,7},{7,8},{8,9},{9,10},{10,1... | collective-permute-start | bytes 3080 | tf_op jit(solution)/shard_map/ppermute | solution.py:31
  91.2 8.6 %collective-permute-start.3 = (f32[2,128]{1,0:T(2,128)S(1)}, f32[2,128]{1,0:T(2,128)S(1)}, u32[]{:S(2)}, u32[]{:S(2)}) collective-permute-start(f32[2,128]{1,0:T(2,128)S(1)} %get-tuple-element.15), channel_id=1, source_target_pairs={{1,0},{2,1},{3,2},{4,3},{5,4},{6,5},{7,6},{8,7},{9,8},{10,9},{11,1... | collective-permute-start | bytes 3080 | tf_op jit(solution)/shard_map/ppermute | solution.py:33
  101.1 8.6 %collective-permute-start.6 = (f32[16,128]{1,0:T(8,128)S(1)}, f32[16,128]{1,0:T(8,128)S(1)}, u32[]{:S(2)}, u32[]{:S(2)}) collective-permute-start(f32[16,128]{1,0:T(8,128)S(1)} %get-tuple-element.22), channel_id=1, source_target_pairs={{0,1},{1,2},{2,3},{3,4},{4,5},{5,6},{6,7},{7,8},{8,9},{9,10},{10,1... | collective-permute-start | bytes 24584 | tf_op jit(solution)/shard_map/ppermute | solution.py:31
  101.2 8.5 %collective-permute-start.7 = (f32[16,128]{1,0:T(8,128)S(1)}, f32[16,128]{1,0:T(8,128)S(1)}, u32[]{:S(2)}, u32[]{:S(2)}) collective-permute-start(f32[16,128]{1,0:T(8,128)S(1)} %get-tuple-element.23), channel_id=1, source_target_pairs={{1,0},{2,1},{3,2},{4,3},{5,4},{6,5},{7,6},{8,7},{9,8},{10,9},{11,1... | collective-permute-start | bytes 24584 | tf_op jit(solution)/shard_map/ppermute | solution.py:33
  149.5 8.8 %collective-permute-start.8 = (f32[16,128]{1,0:T(8,128)S(1)}, f32[16,128]{1,0:T(8,128)S(1)}, u32[]{:S(2)}, u32[]{:S(2)}) collective-permute-start(f32[16,128]{1,0:T(8,128)S(1)} %get-tuple-element.20), channel_id=1, source_target_pairs={{0,1},{1,2},{2,3},{3,4},{4,5},{5,6},{6,7},{7,8},{8,9},{9,10},{10,1... | collective-permute-start | bytes 24584 | tf_op jit(solution)/shard_map/ppermute | solution.py:31
  150.5 7.7 %collective-permute-start.9 = (f32[16,128]{1,0:T(8,128)S(1)}, f32[16,128]{1,0:T(8,128)S(1)}, u32[]{:S(2)}, u32[]{:S(2)}) collective-permute-start(f32[16,128]{1,0:T(8,128)S(1)} %get-tuple-element.21), channel_id=1, source_target_pairs={{1,0},{2,1},{3,2},{4,3},{5,4},{6,5},{7,6},{8,7},{9,8},{10,9},{11,1... | collective-permute-start | bytes 24584 | tf_op jit(solution)/shard_map/ppermute | solution.py:33
  197.1 8.6 %collective-permute-start.10 = (f32[16,128]{1,0:T(8,128)S(1)}, f32[16,128]{1,0:T(8,128)S(1)}, u32[]{:S(2)}, u32[]{:S(2)}) collective-permute-start(f32[16,128]{1,0:T(8,128)S(1)} %get-tuple-element.18), channel_id=1, source_target_pairs={{0,1},{1,2},{2,3},{3,4},{4,5},{5,6},{6,7},{7,8},{8,9},{9,10},{10,1... | collective-permute-start | bytes 24584 | tf_op jit(solution)/shard_map/ppermute | solution.py:31
  198.0 7.7 %collective-permute-start.11 = (f32[16,128]{1,0:T(8,128)S(1)}, f32[16,128]{1,0:T(8,128)S(1)}, u32[]{:S(2)}, u32[]{:S(2)}) collective-permute-start(f32[16,128]{1,0:T(8,128)S(1)} %get-tuple-element.19), channel_id=1, source_target_pairs={{1,0},{2,1},{3,2},{4,3},{5,4},{6,5},{7,6},{8,7},{9,8},{10,9},{11,1... | collective-permute-start | bytes 24584 | tf_op jit(solution)/shard_map/ppermute | solution.py:33
  244.6 8.6 %collective-permute-start.12 = (f32[16,128]{1,0:T(8,128)S(1)}, f32[16,128]{1,0:T(8,128)S(1)}, u32[]{:S(2)}, u32[]{:S(2)}) collective-permute-start(f32[16,128]{1,0:T(8,128)S(1)} %get-tuple-element.16), channel_id=1, source_target_pairs={{0,1},{1,2},{2,3},{3,4},{4,5},{5,6},{6,7},{7,8},{8,9},{9,10},{10,1... | collective-permute-start | bytes 24584 | tf_op jit(solution)/shard_map/ppermute | solution.py:31
  245.5 7.7 %collective-permute-start.13 = (f32[16,128]{1,0:T(8,128)S(1)}, f32[16,128]{1,0:T(8,128)S(1)}, u32[]{:S(2)}, u32[]{:S(2)}) collective-permute-start(f32[16,128]{1,0:T(8,128)S(1)} %get-tuple-element.17), channel_id=1, source_target_pairs={{1,0},{2,1},{3,2},{4,3},{5,4},{6,5},{7,6},{8,7},{9,8},{10,9},{11,1... | collective-permute-start | bytes 24584 | tf_op jit(solution)/shard_map/ppermute | solution.py:33

commit v4 on v3

--- a/solution.py
+++ b/solution.py
@@ -218,29 +218,52 @@
     start_rows = row_start
     grid = ("row", "col")
 
-    def inner_sum(first_field, second_field):
-        return grid_totals([jnp.sum(first_field * second_field)])[0]
-
     fine_rows = start_rows.shape[0]
-    coarse_rows = fine_rows // DEC
     fine_reach = W + DEC * low_reach
-
-    lifting = up_matrix(blur_taps, offsets, coarse_rows + 2 * low_reach, low_reach)
-    lowering = down_matrix(blur_taps, offsets, coarse_rows + 2 * low_reach, fine_rows + 2 * fine_reach)
+    halo = (ITERS + 1) * fine_reach
+    coarse_halo = halo // DEC + low_reach
+    wide_rows = fine_rows + 2 * halo
+    count = lax.axis_size("row") * cols
+    pieces = (start_rows, multi_sums, hyper_sums)
+    reaches = (halo, halo, coarse_halo)
+    tails = jnp.concatenate([piece[piece.shape[0] - reach :] for piece, reach in zip(pieces, reaches)])
+    heads = jnp.concatenate([piece[:reach] for piece, reach in zip(pieces, reaches)])
+    before = lax.ppermute(tails, grid, [(i, (i + 1) % count) for i in range(count)])
+    after = lax.ppermute(heads, grid, [((i + 1) % count, i) for i in range(count)])
+    wide = []
+    corner = 0
+    for piece, reach in zip(pieces, reaches):
+        wide.append(
+            jnp.concatenate(
+                [before[corner : corner + reach], piece, after[corner : corner + reach]]
+            )
+        )
+        corner += reach
+    start_wide, multi_wide, hyper_wide = wide
+
+    lifting = up_matrix(blur_taps, offsets, wide_rows // DEC + 2 * low_reach, low_reach)
+    lowering = down_matrix(
+        blur_taps, offsets, wide_rows // DEC + 2 * low_reach, wide_rows + 2 * fine_reach
+    )
     blurring = jnp.dot(lifting, lowering, precision=FULL_PRECISION)
+    blurring = blurring[:, fine_reach : fine_reach + wide_rows]
 
     def operate(values):
-        fine_wide = extended(values, ((grid, 0),), fine_reach)
-        restored = apply_band(blurring, fine_wide)
+        restored = apply_band(blurring, values)
         return (
             jnp.dot(restored, hyper_gram, precision=FULL_PRECISION)
             + jnp.dot(values, multi_gram, precision=FULL_PRECISION)
             + RIDGE_TERM * values
         )
 
-    hyper_wide = extended(hyper_sums, ((grid, 0),), low_reach)
-    right_side = apply_band(lifting, hyper_wide) + multi_sums
-    solution = start_rows
+    def own(values):
+        return values[halo : halo + fine_rows]
+
+    def inner_sum(first_field, second_field):
+        return grid_totals([jnp.sum(own(first_field) * own(second_field))])[0]
+
+    right_side = apply_band(lifting, hyper_wide) + multi_wide
+    solution = start_wide
     residual = right_side - operate(solution)
     direction = residual
     norm_now = None
@@ -248,7 +271,7 @@
         mapped = operate(direction)
         if norm_now is None:
             norm_now, curvature = grid_totals(
-                [jnp.sum(residual * residual), jnp.sum(direction * mapped)]
+                [jnp.sum(own(residual) * own(residual)), jnp.sum(own(direction) * own(mapped))]
             )
         else:
             curvature = inner_sum(direction, mapped)
@@ -258,6 +281,8 @@
         norm_next = inner_sum(residual, residual)
         direction = residual + norm_next / norm_now * direction
         norm_now = norm_next
+    solution = own(solution)
+    residual = own(residual)
     return (solution, residual)
 
 

time: 293 us -> 263 us (0.90)
  starting transfers between devices: 47.7 us -> 11.6 us
  Pallas kernels: 145 us -> 150 us
  other arithmetic: 8.86 us -> 13.4 us
  waiting for transfers between devices: 5.48 us -> 2.17 us
    ppermute x7 -> x1, starting transfers between devices: 43.3 us -> 2.64 us  [extended(): lax.ppermute(head, axis, [((i + 1) % count, i) for i in range(count)])]
    pallas_call x1, Pallas kernels: 30.3 us -> 40.1 us  [col_scatter(): pl.pallas_call(functools.partial(scatter_kernel, cols), out_shape=(jax.Sh...]
    ppermute x0 -> x2, starting transfers between devices: none -> 7.49 us  [the longest x1 7.41 us: body(): lax.ppermute(heads, grid, [((i + 1) % count, i) for i in range(count)])]
    ppermute x7 -> x1, waiting for transfers between devices: 5.33 us -> 0.01 us  [extended(): lax.ppermute(tail, axis, [(i, (i + 1) % count) for i in range(count)])]
    pallas_call x8, Pallas kernels: 115 us -> 110 us  [grid_totals(): pl.pallas_call(functools.partial(total_kernel, rows, cols), out_shape=jax...]
  transfers between devices with their start and end apart: 14 -> 4, of which waited for: 4 -> 2; matrix products, arithmetic and copies ran while one was open for 8% -> 4% of each run, Pallas kernels for 10% -> 0%
where the time goes in v4:
time: 263 us; the launch traced here: 261 us
  Pallas kernels  150 us (57%)
  blocking collectives  25.9 us (10%)
  matrix products  25.6 us (10%)
  local copies, waits for them, and re-layouts  21.8 us (8%)
  other arithmetic  13.4 us (5%)
  starting transfers between devices  11.6 us (4%)
  between operations  10.4 us (4%)
    pallas_call x8, Pallas kernels, grid_totals(): pl.pallas_call(functools.partial(total_kernel, rows, cols), out_shape=jax...  110 us
    pallas_call x1, Pallas kernels, col_scatter(): pl.pallas_call(functools.partial(scatter_kernel, cols), out_shape=(jax.Sh...  40.1 us
    all_gather x1, blocking collectives, body(): columns = lax.all_gather(col_factor, 'row', axis=1, tiled=True)  25.9 us
    slice x7, local copies, waits for them, and re-layouts, grid_totals(): return [summed[0, number] for number in range(len(parts))]  8.6 us
    dot_general x1, matrix products, body(): jnp.einsum('kij,kjr->ir', hyperspectral, hyper_pairs, preferred_element_t...  7.49 us
    ppermute x1, starting transfers between devices, body(): lax.ppermute(heads, grid, [((i + 1) % count, i) for i in range(count)])  7.41 us
    dot_general x7, matrix products, apply_band(): return jnp.dot(matrix, values.astype(jnp.float32), precision=FULL_PRECISION)  5.98 us
  transfers between devices with their start and end apart: 4, of which 2 were waited for; matrix products, arithmetic and copies ran while one was open for 4% of the time, Pallas kernels for 0%

profile of v4, /device:TPU:0, one launch (start us, length us, event | category | flops | bytes accessed | tf_op | source)
XLA Modules:
  0.0 260.9 jit_solution(11989326486992133169)
XLA Ops:
  0.6 25.9 %all_gather.3 = bf16[512,128]{0,1:T(8,128)(2,1)S(1)} all-gather(bf16[512,8]{0,1:T(8,128)(2,1)} %param.11), channel_id=1, replica_groups=mesh['row'=16,'col'=8] {'row'}, dimensions={1}, use_global_device_ids=true | all-gather | bytes 139264 | tf_op jit(solution)/shard_map/all_gather | solution.py:188
  26.7 1.5 collective-permute-start
  28.2 2.6 %collective-permute-start.1 = (bf16[8,128]{0,1:T(8,128)(2,1)S(1)}, bf16[8,128]{0,1:T(8,128)(2,1)S(1)}, u32[]{:S(2)}, u32[]{:S(2)}) collective-permute-start(bf16[8,128]{0,1:T(8,128)(2,1)S(1)} %get-tuple-element.17), channel_id=1, source_target_pairs={{1,0},{2,1},{3,2},{4,3},{5,4},{6,5},{7,6},{0,7},{9,8},{10,9},{11,1... | collective-permute-start | bytes 6152 | tf_op jit(solution)/shard_map/ppermute | solution.py:33
  31.7 1.4 select_reduce_fusion.1
  36.1 3.7 %convolution_bitcast_fusion = f32[2048,128]{0,1:T(8,128)S(1)} fusion(bf16[2,2048,512]{2,1,0:T(8,128)(2,1)} %param.8, f32[512,128]{0,1:T(8,128)S(1)} %convert_element_type.20, f32[2,128]{1,0:T(2,128)S(1)} %fusion.44), kind=kOutput, calls=%fused_computation.4 | convolution fusion | flops 537133056 | bytes 5506048 | tf_op jit(solution)/shard_map/kij,kjr->ir/dot_general | solution.py:197
  41.3 1.5 fusion.14
  43.2 7.5 %fusion.3 = f32[512,128]{0,1:T(8,128)S(1)} fusion(bf16[96,512,128]{2,1,0:T(8,128)(2,1)} %param.9, f32[128,128]{0,1:T(8,128)S(1)} %copy.14, f32[96,128]{1,0:T(8,128)S(1)} %copy-done.2), kind=kOutput, calls=%fused_computation.12 | convolution fusion | flops 1613758464 | bytes 12959744 | tf_op jit(solution)/shard_map/kij,kjr->ir/dot_general | solution.py:200
  52.7 40.1 %shard_map.95 = (f32[320,128]{1,0:T(8,128)}, f32[256,128]{1,0:T(8,128)}) custom-call(f32[8,320,128]{2,1,0:T(8,128)} %pad_maximum_fusion.blocks_ref, f32[256,128]{1,0:T(8,128)} %pad_maximum_fusion.2.gram_ref), custom_call_target="tpu_custom_call" | custom-call | tf_op jit(solution)/shard_map/pallas_call | solution.py:166
  98.4 7.4 %collective-permute-start.3 = (f32[182,128]{1,0:T(8,128)S(1)}, f32[182,128]{1,0:T(8,128)S(1)}, u32[]{:S(2)}, u32[]{:S(2)}) collective-permute-start(f32[182,128]{1,0:T(8,128)S(1)} %pad_maximum_fusion.4), channel_id=1, source_target_pairs={{1,0},{2,1},{3,2},{4,3},{5,4},{6,5},{7,6},{8,7},{9,8},{10,9},{11,1... | collective-permute-start | bytes 279560 | tf_op jit(solution)/shard_map/ppermute | solution.py:232
  105.8 2.0 collective-permute-done.2
  112.0 1.4 fusion.33
  114.0 15.2 %shard_map.96 = f32[8,128]{1,0:T(8,128)} custom-call(f32[8,128]{1,0:T(8,128)} %broadcast_in_dim.58.part_ref), custom_call_target="tpu_custom_call" | custom-call | tf_op jit(solution)/shard_map/pallas_call | solution.py:112
  129.2 1.3 fusion.43
  133.8 13.5 %shard_map.97 = f32[8,128]{1,0:T(8,128)} custom-call(f32[8,128]{1,0:T(8,128)} %broadcast_in_dim.59.part_ref), custom_call_target="tpu_custom_call" | custom-call | tf_op jit(solution)/shard_map/pallas_call | solution.py:112
  147.4 1.3 slice.155
  153.4 13.3 %shard_map.98 = f32[8,128]{1,0:T(8,128)} custom-call(f32[8,128]{1,0:T(8,128)} %broadcast_in_dim.60.part_ref), custom_call_target="tpu_custom_call" | custom-call | tf_op jit(solution)/shard_map/pallas_call | solution.py:112
  166.7 1.2 slice.158
  171.1 14.0 %shard_map.99 = f32[8,128]{1,0:T(8,128)} custom-call(f32[8,128]{1,0:T(8,128)} %broadcast_in_dim.61.part_ref), custom_call_target="tpu_custom_call" | custom-call | tf_op jit(solution)/shard_map/pallas_call | solution.py:112
  191.1 12.8 %shard_map.100 = f32[8,128]{1,0:T(8,128)} custom-call(f32[8,128]{1,0:T(8,128)} %broadcast_in_dim.62.part_ref), custom_call_target="tpu_custom_call" | custom-call | tf_op jit(solution)/shard_map/pallas_call | solution.py:112
  208.4 14.0 %shard_map.101 = f32[8,128]{1,0:T(8,128)} custom-call(f32[8,128]{1,0:T(8,128)} %broadcast_in_dim.63.part_ref), custom_call_target="tpu_custom_call" | custom-call | tf_op jit(solution)/shard_map/pallas_call | solution.py:112
  222.4 1.2 slice.165
  228.3 12.8 %shard_map.102 = f32[8,128]{1,0:T(8,128)} custom-call(f32[8,128]{1,0:T(8,128)} %broadcast_in_dim.64.part_ref), custom_call_target="tpu_custom_call" | custom-call | tf_op jit(solution)/shard_map/pallas_call | solution.py:112
  243.7 1.3 multiply_reduce_fusion
  246.2 14.0 %shard_map.103 = f32[8,128]{1,0:T(8,128)} custom-call(f32[8,128]{1,0:T(8,128)} %broadcast_in_dim.65.part_ref), custom_call_target="tpu_custom_call" | custom-call | tf_op jit(solution)/shard_map/pallas_call | solution.py:112
  (93 shorter events, 39.4 us)
Async XLA Ops:
  0.6 33.5 %copy-start = (f32[2,96]{1,0:T(2,128)S(1)}, f32[2,96]{1,0:T(2,128)}, u32[]{:S(2)}) copy-start(f32[2,96]{1,0:T(2,128)} %param.13) | copy-start | bytes 2308
  26.7 14.6 %collective-permute-start = (bf16[8,128]{0,1:T(8,128)(2,1)S(1)}, bf16[8,128]{0,1:T(8,128)(2,1)S(1)}, u32[]{:S(2)}, u32[]{:S(2)}) collective-permute-start(bf16[8,128]{0,1:T(8,128)(2,1)S(1)} %get-tuple-element.16), channel_id=1, source_target_pairs={{0,1},{1,2},{2,3},{3,4},{4,5},{5,6},{6,7},{7,0},{8,9},{9,10},{10,1... | collective-permute-start | bytes 6152 | tf_op jit(solution)/shard_map/ppermute | solution.py:31
  28.2 13.1 %collective-permute-start.1 = (bf16[8,128]{0,1:T(8,128)(2,1)S(1)}, bf16[8,128]{0,1:T(8,128)(2,1)S(1)}, u32[]{:S(2)}, u32[]{:S(2)}) collective-permute-start(bf16[8,128]{0,1:T(8,128)(2,1)S(1)} %get-tuple-element.17), channel_id=1, source_target_pairs={{1,0},{2,1},{3,2},{4,3},{5,4},{6,5},{7,6},{0,7},{9,8},{10,9},{11,1... | collective-permute-start | bytes 6152 | tf_op jit(solution)/shard_map/ppermute | solution.py:33
  36.1 3.7 %copy-start.4 = (f32[9]{0:T(128)S(1)}, f32[9]{0:T(128)}, u32[]{:S(2)}) copy-start(f32[9]{0:T(128)} %param.14) | copy-start | bytes 112
  36.1 3.7 %copy-start.5 = (s32[9]{0:T(128)S(1)}, s32[9]{0:T(128)}, u32[]{:S(2)}) copy-start(s32[9]{0:T(128)} %param.15) | copy-start | bytes 112
  39.8 3.4 %copy-start.2 = (f32[96,128]{1,0:T(8,128)S(1)}, f32[96,128]{1,0:T(8,128)}, u32[]{:S(2)}) copy-start(f32[96,128]{1,0:T(8,128)} %param.12) | copy-start | bytes 147460
  50.7 1.3 copy-start.3
  50.8 46.7 %copy-start.1 = (f32[256,128]{1,0:T(8,128)S(1)}, f32[256,128]{1,0:T(8,128)}, u32[]{:S(2)}) copy-start(f32[256,128]{1,0:T(8,128)} %param.10) | copy-start | bytes 393220
  98.3 9.5 %collective-permute-start.2 = (f32[182,128]{1,0:T(8,128)S(1)}, f32[182,128]{1,0:T(8,128)S(1)}, u32[]{:S(2)}, u32[]{:S(2)}) collective-permute-start(f32[182,128]{1,0:T(8,128)S(1)} %pad_maximum_fusion.3), channel_id=1, source_target_pairs={{0,1},{1,2},{2,3},{3,4},{4,5},{5,6},{6,7},{7,8},{8,9},{9,10},{10,1... | collective-permute-start | bytes 279560 | tf_op jit(solution)/shard_map/ppermute | solution.py:231
  98.4 9.6 %collective-permute-start.3 = (f32[182,128]{1,0:T(8,128)S(1)}, f32[182,128]{1,0:T(8,128)S(1)}, u32[]{:S(2)}, u32[]{:S(2)}) collective-permute-start(f32[182,128]{1,0:T(8,128)S(1)} %pad_maximum_fusion.4), channel_id=1, source_target_pairs={{1,0},{2,1},{3,2},{4,3},{5,4},{6,5},{7,6},{8,7},{9,8},{10,9},{11,1... | collective-permute-start | bytes 279560 | tf_op jit(solution)/shard_map/ppermute | solution.py:232

commit v5 on v4

--- a/solution.py
+++ b/solution.py
@@ -181,11 +181,53 @@
     )(blocks, gram)
 
 
+def gather_kernel(rows, piece_ref, out_ref, sends, receipts):
+    here_row = lax.axis_index("row")
+    here_col = lax.axis_index("col")
+    peers = [(lax.rem(here_row + shift, rows), here_col) for shift in range(1, rows)]
+    barrier = pltpu.get_barrier_semaphore()
+    for peer in peers:
+        pl.semaphore_signal(barrier, inc=1, device_id=peer, device_id_type=MESH)
+    pl.semaphore_wait(barrier, len(peers))
+    copies = []
+    for number, peer in enumerate(peers):
+        copy = pltpu.make_async_remote_copy(
+            src_ref=piece_ref,
+            dst_ref=out_ref.at[here_row],
+            send_sem=sends.at[number],
+            recv_sem=receipts.at[number],
+            device_id=peer,
+            device_id_type=MESH,
+        )
+        copy.start()
+        copies.append(copy)
+    out_ref[here_row] = piece_ref[...]
+    for copy in copies:
+        copy.wait()
+
+
+def row_gather(piece):
+    rows = lax.axis_size("row")
+    flipped = piece.T.astype(jnp.float32)
+    gathered = pl.pallas_call(
+        functools.partial(gather_kernel, rows),
+        out_shape=jax.ShapeDtypeStruct((rows,) + flipped.shape, jnp.float32),
+        in_specs=[pl.BlockSpec(memory_space=pltpu.VMEM)],
+        out_specs=pl.BlockSpec(memory_space=pltpu.VMEM),
+        scratch_shapes=[
+            pltpu.SemaphoreType.DMA((rows,)),
+            pltpu.SemaphoreType.DMA((rows,)),
+        ],
+        compiler_params=pltpu.CompilerParams(collective_id=2, has_side_effects=True),
+    )(flipped)
+    return gathered.reshape(-1, flipped.shape[1]).T.astype(piece.dtype)
+
+
 def body(
     multispectral, hyperspectral, row_start, col_factor, band_factor, response, blur_taps, offsets
 ):
     low_reach = (W + DEC - 1) // DEC
-    columns = lax.all_gather(col_factor, "row", axis=1, tiled=True)
+    columns = row_gather(col_factor)
     column_wide = extended(columns, (("col", 0),), W)
     column_down = down_matrix(blur_taps, offsets, columns.shape[0] // DEC, column_wide.shape[0])
     coarse_columns = apply_band(column_down, column_wide)

time: 263 us -> 252 us (0.958)
  blocking collectives: 25.9 us -> 0 us
  Pallas kernels: 150 us -> 162 us
    all_gather x1 -> x0, blocking collectives: 25.9 us -> none  [body(): columns = lax.all_gather(col_factor, 'row', axis=1, tiled=True)]
    pallas_call x0 -> x1, Pallas kernels: none -> 13.2 us  [row_gather(): pl.pallas_call(functools.partial(gather_kernel, rows), out_shape=jax.Shap...]
where the time goes in v5:
time: 252 us; the launch traced here: 250 us
  Pallas kernels  162 us (64%)
  matrix products  26.7 us (11%)
  local copies, waits for them, and re-layouts  21.8 us (9%)
  other arithmetic  15 us (6%)
  starting transfers between devices  11.6 us (5%)
  between operations  10.5 us (4%)
    pallas_call x8, Pallas kernels, grid_totals(): pl.pallas_call(functools.partial(total_kernel, rows, cols), out_shape=jax...  110 us
    pallas_call x1, Pallas kernels, col_scatter(): pl.pallas_call(functools.partial(scatter_kernel, cols), out_shape=(jax.Sh...  38.9 us
    pallas_call x1, Pallas kernels, row_gather(): pl.pallas_call(functools.partial(gather_kernel, rows), out_shape=jax.Shap...  13.2 us
    slice x7, local copies, waits for them, and re-layouts, grid_totals(): return [summed[0, number] for number in range(len(parts))]  8.6 us
    dot_general x1, matrix products, body(): jnp.einsum('kij,kjr->ir', hyperspectral, hyper_pairs, preferred_element_t...  7.53 us
    ppermute x1, starting transfers between devices, body(): lax.ppermute(heads, grid, [((i + 1) % count, i) for i in range(count)])  7.41 us
    dot_general x7, matrix products, apply_band(): return jnp.dot(matrix, values.astype(jnp.float32), precision=FULL_PRECISION)  5.95 us
    reduce_sum x7, other arithmetic, inner_sum(): return grid_totals([jnp.sum(own(first_field) * own(second_field))])[0]  5.07 us
  transfers between devices with their start and end apart: 4, of which 2 were waited for; matrix products, arithmetic and copies ran while one was open for 4% of the time, Pallas kernels for 0%

profile of v5, /device:TPU:0, one launch (start us, length us, event | category | flops | bytes accessed | tf_op | source)
XLA Modules:
  0.0 249.6 jit_solution(16524394711311370979)
XLA Ops:
  0.6 1.3 convert_bitcast_fusion.1.piece_ref
  2.0 13.2 %shard_map.95 = f32[16,8,512]{2,1,0:T(8,128)} custom-call(f32[8,512]{1,0:T(8,128)} %convert_bitcast_fusion.1.piece_ref), custom_call_target="tpu_custom_call" | custom-call | tf_op jit(solution)/shard_map/pallas_call | solution.py:212
  16.2 1.5 collective-permute-start
  17.8 2.6 %collective-permute-start.1 = (bf16[8,128]{0,1:T(8,128)(2,1)S(1)}, bf16[8,128]{0,1:T(8,128)(2,1)}, u32[]{:S(2)}, u32[]{:S(2)}) collective-permute-start(bf16[8,128]{0,1:T(8,128)(2,1)S(1)} %get-tuple-element.19), channel_id=1, source_target_pairs={{1,0},{2,1},{3,2},{4,3},{5,4},{6,5},{7,6},{0,7},{9,8},{10,9},{11,1... | collective-permute-start | bytes 6152 | tf_op jit(solution)/shard_map/ppermute | solution.py:33
  20.4 1.9 fusion.28
  22.3 1.4 select_reduce_fusion.1
  26.7 3.7 %convolution_bitcast_fusion = f32[2048,128]{0,1:T(8,128)S(1)} fusion(bf16[2,2048,512]{2,1,0:T(8,128)(2,1)} %param.8, f32[512,128]{0,1:T(8,128)S(1)} %get-tuple-element.10, f32[2,128]{1,0:T(2,128)S(1)} %fusion.48), kind=kOutput, calls=%fused_computation.4 | convolution fusion | flops 537133056 | bytes 5506048 | tf_op jit(solution)/shard_map/kij,kjr->ir/dot_general | solution.py:239
  31.2 1.4 fusion.14
  33.1 7.5 %fusion.3 = f32[512,128]{0,1:T(8,128)S(1)} fusion(bf16[96,512,128]{2,1,0:T(8,128)(2,1)} %param.9, f32[128,128]{0,1:T(8,128)S(1)} %copy.14, f32[96,128]{1,0:T(8,128)} %param.12), kind=kOutput, calls=%fused_computation.12 | convolution fusion | flops 1613758464 | bytes 12959744 | tf_op jit(solution)/shard_map/kij,kjr->ir/dot_general | solution.py:242
  42.6 38.9 %shard_map.96 = (f32[320,128]{1,0:T(8,128)}, f32[256,128]{1,0:T(8,128)}) custom-call(f32[8,320,128]{2,1,0:T(8,128)} %pad_maximum_fusion.blocks_ref, f32[256,128]{1,0:T(8,128)} %pad_maximum_fusion.2.gram_ref), custom_call_target="tpu_custom_call" | custom-call | tf_op jit(solution)/shard_map/pallas_call | solution.py:166
  87.1 7.4 %collective-permute-start.3 = (f32[182,128]{1,0:T(8,128)S(1)}, f32[182,128]{1,0:T(8,128)S(1)}, u32[]{:S(2)}, u32[]{:S(2)}) collective-permute-start(f32[182,128]{1,0:T(8,128)S(1)} %pad_maximum_fusion.4), channel_id=1, source_target_pairs={{1,0},{2,1},{3,2},{4,3},{5,4},{6,5},{7,6},{8,7},{9,8},{10,9},{11,1... | collective-permute-start | bytes 279560 | tf_op jit(solution)/shard_map/ppermute | solution.py:274
  94.5 2.0 collective-permute-done.2
  100.8 1.4 fusion.36
  102.7 15.8 %shard_map.97 = f32[8,128]{1,0:T(8,128)} custom-call(f32[8,128]{1,0:T(8,128)} %broadcast_in_dim.58.part_ref), custom_call_target="tpu_custom_call" | custom-call | tf_op jit(solution)/shard_map/pallas_call | solution.py:112
  118.5 1.3 fusion.47
  123.1 13.0 %shard_map.98 = f32[8,128]{1,0:T(8,128)} custom-call(f32[8,128]{1,0:T(8,128)} %broadcast_in_dim.59.part_ref), custom_call_target="tpu_custom_call" | custom-call | tf_op jit(solution)/shard_map/pallas_call | solution.py:112
  136.1 1.3 slice.155
  142.1 13.7 %shard_map.99 = f32[8,128]{1,0:T(8,128)} custom-call(f32[8,128]{1,0:T(8,128)} %broadcast_in_dim.60.part_ref), custom_call_target="tpu_custom_call" | custom-call | tf_op jit(solution)/shard_map/pallas_call | solution.py:112
  160.3 13.6 %shard_map.100 = f32[8,128]{1,0:T(8,128)} custom-call(f32[8,128]{1,0:T(8,128)} %broadcast_in_dim.61.part_ref), custom_call_target="tpu_custom_call" | custom-call | tf_op jit(solution)/shard_map/pallas_call | solution.py:112
  179.8 13.1 %shard_map.101 = f32[8,128]{1,0:T(8,128)} custom-call(f32[8,128]{1,0:T(8,128)} %broadcast_in_dim.62.part_ref), custom_call_target="tpu_custom_call" | custom-call | tf_op jit(solution)/shard_map/pallas_call | solution.py:112
  197.4 13.7 %shard_map.102 = f32[8,128]{1,0:T(8,128)} custom-call(f32[8,128]{1,0:T(8,128)} %broadcast_in_dim.63.part_ref), custom_call_target="tpu_custom_call" | custom-call | tf_op jit(solution)/shard_map/pallas_call | solution.py:112
  217.1 13.1 %shard_map.103 = f32[8,128]{1,0:T(8,128)} custom-call(f32[8,128]{1,0:T(8,128)} %broadcast_in_dim.64.part_ref), custom_call_target="tpu_custom_call" | custom-call | tf_op jit(solution)/shard_map/pallas_call | solution.py:112
  232.7 1.3 multiply_reduce_fusion
  235.2 13.7 %shard_map.104 = f32[8,128]{1,0:T(8,128)} custom-call(f32[8,128]{1,0:T(8,128)} %broadcast_in_dim.65.part_ref), custom_call_target="tpu_custom_call" | custom-call | tf_op jit(solution)/shard_map/pallas_call | solution.py:112
  (96 shorter events, 41.3 us)
Async XLA Ops:
  0.6 24.1 %copy-start = (f32[2,96]{1,0:T(2,128)S(1)}, f32[2,96]{1,0:T(2,128)}, u32[]{:S(2)}) copy-start(f32[2,96]{1,0:T(2,128)} %param.13) | copy-start | bytes 2308
  16.2 6.1 %copy-start.2 = (bf16[512,128]{0,1:T(8,128)(2,1)}, bf16[512,128]{0,1:T(8,128)(2,1)S(1)}, u32[]{:S(2)}) copy-start(bf16[512,128]{0,1:T(8,128)(2,1)S(1)} %get-tuple-element.11) | copy-start | bytes 393220
  16.2 14.9 %collective-permute-start = (bf16[8,128]{0,1:T(8,128)(2,1)S(1)}, bf16[8,128]{0,1:T(8,128)(2,1)S(1)}, u32[]{:S(2)}, u32[]{:S(2)}) collective-permute-start(bf16[8,128]{0,1:T(8,128)(2,1)S(1)} %get-tuple-element.18), channel_id=1, source_target_pairs={{0,1},{1,2},{2,3},{3,4},{4,5},{5,6},{6,7},{7,0},{8,9},{9,10},{10,1... | collective-permute-start | bytes 6152 | tf_op jit(solution)/shard_map/ppermute | solution.py:31
  17.8 13.4 %collective-permute-start.1 = (bf16[8,128]{0,1:T(8,128)(2,1)S(1)}, bf16[8,128]{0,1:T(8,128)(2,1)}, u32[]{:S(2)}, u32[]{:S(2)}) collective-permute-start(bf16[8,128]{0,1:T(8,128)(2,1)S(1)} %get-tuple-element.19), channel_id=1, source_target_pairs={{1,0},{2,1},{3,2},{4,3},{5,4},{6,5},{7,6},{0,7},{9,8},{10,9},{11,1... | collective-permute-start | bytes 6152 | tf_op jit(solution)/shard_map/ppermute | solution.py:33
  26.7 3.7 %copy-start.5 = (f32[9]{0:T(128)S(1)}, f32[9]{0:T(128)}, u32[]{:S(2)}) copy-start(f32[9]{0:T(128)} %param.14) | copy-start | bytes 112
  26.7 3.7 %copy-start.6 = (s32[9]{0:T(128)S(1)}, s32[9]{0:T(128)}, u32[]{:S(2)}) copy-start(s32[9]{0:T(128)} %param.15) | copy-start | bytes 112
  40.6 1.3 copy-start.4
  40.6 40.9 %copy-start.3 = (f32[96,128]{1,0:T(8,128)S(1)}, f32[96,128]{1,0:T(8,128)}, u32[]{:S(2)}) copy-start(f32[96,128]{1,0:T(8,128)} %param.12) | copy-start | bytes 147460
  40.7 45.5 %copy-start.1 = (f32[256,128]{1,0:T(8,128)S(1)}, f32[256,128]{1,0:T(8,128)}, u32[]{:S(2)}) copy-start(f32[256,128]{1,0:T(8,128)} %param.10) | copy-start | bytes 393220
  87.0 9.5 %collective-permute-start.2 = (f32[182,128]{1,0:T(8,128)S(1)}, f32[182,128]{1,0:T(8,128)S(1)}, u32[]{:S(2)}, u32[]{:S(2)}) collective-permute-start(f32[182,128]{1,0:T(8,128)S(1)} %pad_maximum_fusion.3), channel_id=1, source_target_pairs={{0,1},{1,2},{2,3},{3,4},{4,5},{5,6},{6,7},{7,8},{8,9},{9,10},{10,1... | collective-permute-start | bytes 279560 | tf_op jit(solution)/shard_map/ppermute | solution.py:273
  87.1 9.6 %collective-permute-start.3 = (f32[182,128]{1,0:T(8,128)S(1)}, f32[182,128]{1,0:T(8,128)S(1)}, u32[]{:S(2)}, u32[]{:S(2)}) collective-permute-start(f32[182,128]{1,0:T(8,128)S(1)} %pad_maximum_fusion.4), channel_id=1, source_target_pairs={{1,0},{2,1},{3,2},{4,3},{5,4},{6,5},{7,6},{8,7},{9,8},{10,9},{11,1... | collective-permute-start | bytes 279560 | tf_op jit(solution)/shard_map/ppermute | solution.py:274

commit v6 on v5

--- a/solution.py
+++ b/solution.py
@@ -301,9 +301,6 @@
     def own(values):
         return values[halo : halo + fine_rows]
 
-    def inner_sum(first_field, second_field):
-        return grid_totals([jnp.sum(own(first_field) * own(second_field))])[0]
-
     right_side = apply_band(lifting, hyper_wide) + multi_wide
     solution = start_wide
     residual = right_side - operate(solution)
@@ -311,16 +308,20 @@
     norm_now = None
     for iteration in range(ITERS):
         mapped = operate(direction)
+        parts = [
+            jnp.sum(own(direction) * own(mapped)),
+            jnp.sum(own(residual) * own(mapped)),
+            jnp.sum(own(mapped) * own(mapped)),
+        ]
         if norm_now is None:
-            norm_now, curvature = grid_totals(
-                [jnp.sum(own(residual) * own(residual)), jnp.sum(own(direction) * own(mapped))]
-            )
+            parts.append(jnp.sum(own(residual) * own(residual)))
+            curvature, cross, power, norm_now = grid_totals(parts)
         else:
-            curvature = inner_sum(direction, mapped)
+            curvature, cross, power = grid_totals(parts)
         step_size = norm_now / curvature
         solution = solution + step_size * direction
         residual = residual - step_size * mapped
-        norm_next = inner_sum(residual, residual)
+        norm_next = norm_now - 2 * step_size * cross + step_size * step_size * power
         direction = residual + norm_next / norm_now * direction
         norm_now = norm_next
     solution = own(solution)

time: 252 us -> 193 us (0.77)
  Pallas kernels: 162 us -> 108 us
  local copies, waits for them, and re-layouts: 21.8 us -> 12.3 us
  other arithmetic: 15 us -> 20.4 us
    pallas_call x8 -> x4, Pallas kernels: 110 us -> 56.1 us  [grid_totals(): pl.pallas_call(functools.partial(total_kernel, rows, cols), out_shape=jax...]
    another operation x1 -> x4, other arithmetic: 1.37 us -> 8.23 us  [grid_totals(): lanes = jnp.pad(jnp.stack(parts), (0, 128 - len(parts)))]
    pad x7 -> x0, local copies, waits for them, and re-layouts: 4.53 us -> none  [grid_totals(): lanes = jnp.pad(jnp.stack(parts), (0, 128 - len(parts)))]
    slice x7 -> x4, local copies, waits for them, and re-layouts: 8.6 us -> 5.41 us  [grid_totals(): return [summed[0, number] for number in range(len(parts))]]
    reduce_sum x8 -> x4, other arithmetic: 5.7 us -> 2.91 us  [body(): jnp.sum(own(direction) * own(mapped))]
  transfers between devices with their start and end apart: 4 -> 4, of which waited for: 2 -> 2; matrix products, arithmetic and copies ran while one was open for 4% -> 6% of each run, Pallas kernels for 0% -> 0%
where the time goes in v6:
time: 193 us; the launch traced here: 190 us
  Pallas kernels  108 us (56%)
  matrix products  26.1 us (14%)
  other arithmetic  20.4 us (11%)
  local copies, waits for them, and re-layouts  12.3 us (6%)
  starting transfers between devices  11.6 us (6%)
  between operations  9.58 us (5%)
  waiting for transfers between devices  2.17 us (1%)
    pallas_call x4, Pallas kernels, grid_totals(): pl.pallas_call(functools.partial(total_kernel, rows, cols), out_shape=jax...  56.1 us
    pallas_call x1, Pallas kernels, col_scatter(): pl.pallas_call(functools.partial(scatter_kernel, cols), out_shape=(jax.Sh...  38.9 us
    pallas_call x1, Pallas kernels, row_gather(): pl.pallas_call(functools.partial(gather_kernel, rows), out_shape=jax.Shap...  13.2 us
    another operation x4, other arithmetic, grid_totals(): lanes = jnp.pad(jnp.stack(parts), (0, 128 - len(parts)))  8.23 us
    dot_general x1, matrix products, body(): jnp.einsum('kij,kjr->ir', hyperspectral, hyper_pairs, preferred_element_t...  7.5 us
    ppermute x1, starting transfers between devices, body(): lax.ppermute(heads, grid, [((i + 1) % count, i) for i in range(count)])  7.41 us
    dot_general x7, matrix products, apply_band(): return jnp.dot(matrix, values.astype(jnp.float32), precision=FULL_PRECISION)  5.96 us
    slice x4, local copies, waits for them, and re-layouts, grid_totals(): return [summed[0, number] for number in range(len(parts))]  5.41 us
  transfers between devices with their start and end apart: 4, of which 2 were waited for; matrix products, arithmetic and copies ran while one was open for 6% of the time, Pallas kernels for 0%

profile of v6, /device:TPU:0, one launch (start us, length us, event | category | flops | bytes accessed | tf_op | source)
XLA Modules:
  0.0 190.5 jit_solution(10586519573251700884)
XLA Ops:
  0.6 1.3 convert_bitcast_fusion.1.piece_ref
  2.0 13.2 %shard_map.95 = f32[16,8,512]{2,1,0:T(8,128)} custom-call(f32[8,512]{1,0:T(8,128)} %convert_bitcast_fusion.1.piece_ref), custom_call_target="tpu_custom_call" | custom-call | tf_op jit(solution)/shard_map/pallas_call | solution.py:212
  16.9 1.5 collective-permute-start
  18.4 2.6 %collective-permute-start.1 = (bf16[8,128]{0,1:T(8,128)(2,1)}, bf16[8,128]{0,1:T(8,128)(2,1)}, u32[]{:S(2)}, u32[]{:S(2)}) collective-permute-start(bf16[8,128]{0,1:T(8,128)(2,1)} %get-tuple-element.33), channel_id=1, source_target_pairs={{1,0},{2,1},{3,2},{4,3},{5,4},{6,5},{7,6},{0,7},{9,8},{10,9},{11,1... | collective-permute-start | bytes 6152 | tf_op jit(solution)/shard_map/ppermute | solution.py:33
  21.0 1.2 fusion.25
  22.2 1.4 select_reduce_fusion.1
  26.7 3.7 %convolution_bitcast_fusion = f32[2048,128]{0,1:T(8,128)S(1)} fusion(bf16[2,2048,512]{2,1,0:T(8,128)(2,1)} %param.8, f32[512,128]{0,1:T(8,128)S(1)} %get-tuple-element.24, f32[2,128]{1,0:T(2,128)S(1)} %fusion.46), kind=kOutput, calls=%fused_computation.4 | convolution fusion | flops 537133056 | bytes 5506048 | tf_op jit(solution)/shard_map/kij,kjr->ir/dot_general | solution.py:239
  32.0 1.5 fusion.14
  33.9 7.5 %fusion.3 = f32[512,128]{0,1:T(8,128)S(1)} fusion(bf16[96,512,128]{2,1,0:T(8,128)(2,1)} %param.9, f32[128,128]{0,1:T(8,128)S(1)} %copy.14, f32[96,128]{1,0:T(8,128)S(1)} %copy-done.6), kind=kOutput, calls=%fused_computation.12 | convolution fusion | flops 1613758464 | bytes 12959744 | tf_op jit(solution)/shard_map/kij,kjr->ir/dot_general | solution.py:242
  43.3 38.9 %shard_map.96 = (f32[320,128]{1,0:T(8,128)}, f32[256,128]{1,0:T(8,128)}) custom-call(f32[8,320,128]{2,1,0:T(8,128)} %pad_maximum_fusion.blocks_ref, f32[256,128]{1,0:T(8,128)} %pad_maximum_fusion.2.gram_ref), custom_call_target="tpu_custom_call" | custom-call | tf_op jit(solution)/shard_map/pallas_call | solution.py:166
  87.9 7.4 %collective-permute-start.3 = (f32[182,128]{1,0:T(8,128)S(1)}, f32[182,128]{1,0:T(8,128)S(1)}, u32[]{:S(2)}, u32[]{:S(2)}) collective-permute-start(f32[182,128]{1,0:T(8,128)S(1)} %pad_maximum_fusion.4), channel_id=1, source_target_pairs={{1,0},{2,1},{3,2},{4,3},{5,4},{6,5},{7,6},{8,7},{9,8},{10,9},{11,1... | collective-permute-start | bytes 279560 | tf_op jit(solution)/shard_map/ppermute | solution.py:274
  95.3 2.0 %collective-permute-done.2 = f32[182,128]{1,0:T(8,128)S(1)} collective-permute-done((f32[182,128]{1,0:T(8,128)S(1)}, f32[182,128]{1,0:T(8,128)S(1)}, u32[]{:S(2)}, u32[]{:S(2)}) %collective-permute-start.2) | collective-permute-done | bytes 93216 | tf_op jit(solution)/shard_map/ppermute | solution.py:273
  101.6 2.1 %select_maximum_fusion.6 = f32[128]{0:T(128)S(1)} fusion(f32[1]{0:T(128)} %bitcast.12, f32[1]{0:T(128)} %bitcast.11, f32[1]{0:T(128)} %bitcast.10), kind=kLoop, calls=%fused_computation.85 | loop fusion | flops 1024 | bytes 524 | tf_op jit(solution)/shard_map/stack | solution.py:110
  104.3 15.8 %shard_map.97 = f32[8,128]{1,0:T(8,128)} custom-call(f32[8,128]{1,0:T(8,128)} %broadcast_in_dim.76.part_ref), custom_call_target="tpu_custom_call" | custom-call | tf_op jit(solution)/shard_map/pallas_call | solution.py:112
  120.1 1.4 fusion.45
  127.7 2.1 %select_maximum_fusion.4 = f32[128]{0:T(128)S(1)} fusion(f32[1]{0:T(128)} %bitcast.19, f32[1]{0:T(128)} %bitcast.18, f32[1]{0:T(128)} %bitcast.17), kind=kLoop, calls=%fused_computation.82 | loop fusion | flops 768 | bytes 524 | tf_op jit(solution)/shard_map/stack | solution.py:110
  130.3 13.0 %shard_map.98 = f32[8,128]{1,0:T(8,128)} custom-call(f32[8,128]{1,0:T(8,128)} %broadcast_in_dim.77.part_ref), custom_call_target="tpu_custom_call" | custom-call | tf_op jit(solution)/shard_map/pallas_call | solution.py:112
  143.3 1.4 fusion.44
  148.9 2.1 %select_maximum_fusion.2 = f32[128]{0:T(128)S(1)} fusion(f32[1]{0:T(128)} %bitcast.25, f32[1]{0:T(128)} %bitcast.24, f32[1]{0:T(128)} %bitcast.23), kind=kLoop, calls=%fused_computation.80 | loop fusion | flops 768 | bytes 524 | tf_op jit(solution)/shard_map/stack | solution.py:110
  151.6 13.7 %shard_map.99 = f32[8,128]{1,0:T(8,128)} custom-call(f32[8,128]{1,0:T(8,128)} %broadcast_in_dim.78.part_ref), custom_call_target="tpu_custom_call" | custom-call | tf_op jit(solution)/shard_map/pallas_call | solution.py:112
  165.3 1.4 fusion.43
  170.9 2.1 %select_maximum_fusion = f32[128]{0:T(128)S(1)} fusion(f32[1]{0:T(128)} %bitcast.31, f32[1]{0:T(128)} %bitcast.30, f32[1]{0:T(128)} %bitcast.29), kind=kLoop, calls=%fused_computation.78 | loop fusion | flops 768 | bytes 524 | tf_op jit(solution)/shard_map/stack | solution.py:110
  173.6 13.6 %shard_map.100 = f32[8,128]{1,0:T(8,128)} custom-call(f32[8,128]{1,0:T(8,128)} %broadcast_in_dim.79.part_ref), custom_call_target="tpu_custom_call" | custom-call | tf_op jit(solution)/shard_map/pallas_call | solution.py:112
  187.2 1.2 slice.188
  (79 shorter events, 28.9 us)
Async XLA Ops:
  0.6 24.1 %copy-start = (f32[2,96]{1,0:T(2,128)S(1)}, f32[2,96]{1,0:T(2,128)}, u32[]{:S(2)}) copy-start(f32[2,96]{1,0:T(2,128)} %param.13) | copy-start | bytes 2308
  16.2 8.6 %copy-start.4 = (bf16[512,128]{0,1:T(8,128)(2,1)}, bf16[512,128]{0,1:T(8,128)(2,1)S(1)}, u32[]{:S(2)}) copy-start(bf16[512,128]{0,1:T(8,128)(2,1)S(1)} %get-tuple-element.25) | copy-start | bytes 393220
  16.9 15.1 %collective-permute-start = (bf16[8,128]{0,1:T(8,128)(2,1)}, bf16[8,128]{0,1:T(8,128)(2,1)S(1)}, u32[]{:S(2)}, u32[]{:S(2)}) collective-permute-start(bf16[8,128]{0,1:T(8,128)(2,1)} %get-tuple-element.32), channel_id=1, source_target_pairs={{0,1},{1,2},{2,3},{3,4},{4,5},{5,6},{6,7},{7,0},{8,9},{9,10},{10,1... | collective-permute-start | bytes 6152 | tf_op jit(solution)/shard_map/ppermute | solution.py:31
  18.4 13.6 %collective-permute-start.1 = (bf16[8,128]{0,1:T(8,128)(2,1)}, bf16[8,128]{0,1:T(8,128)(2,1)}, u32[]{:S(2)}, u32[]{:S(2)}) collective-permute-start(bf16[8,128]{0,1:T(8,128)(2,1)} %get-tuple-element.33), channel_id=1, source_target_pairs={{1,0},{2,1},{3,2},{4,3},{5,4},{6,5},{7,6},{0,7},{9,8},{10,9},{11,1... | collective-permute-start | bytes 6152 | tf_op jit(solution)/shard_map/ppermute | solution.py:33
  24.8 5.7 %copy-start.2 = (f32[416,108]{1,0:T(8,128)}, f32[416,108]{1,0:T(8,128)S(1)}, u32[]{:S(2)}) copy-start(f32[416,108]{1,0:T(8,128)S(1)} %select_reduce_fusion.2) | copy-start | bytes 539140
  26.7 3.7 %copy-start.7 = (f32[9]{0:T(128)S(1)}, f32[9]{0:T(128)}, u32[]{:S(2)}) copy-start(f32[9]{0:T(128)} %param.14) | copy-start | bytes 112
  26.7 3.7 %copy-start.8 = (s32[9]{0:T(128)S(1)}, s32[9]{0:T(128)}, u32[]{:S(2)}) copy-start(s32[9]{0:T(128)} %param.15) | copy-start | bytes 112
  30.4 1.5 copy-start.5
  30.5 3.4 %copy-start.6 = (f32[96,128]{1,0:T(8,128)S(1)}, f32[96,128]{1,0:T(8,128)}, u32[]{:S(2)}) copy-start(f32[96,128]{1,0:T(8,128)} %param.12) | copy-start | bytes 147460
  41.5 45.5 %copy-start.1 = (f32[256,128]{1,0:T(8,128)S(1)}, f32[256,128]{1,0:T(8,128)}, u32[]{:S(2)}) copy-start(f32[256,128]{1,0:T(8,128)} %param.10) | copy-start | bytes 393220
  82.3 16.8 %copy-start.3 = (f32[416,108]{1,0:T(8,128)S(1)}, f32[416,108]{1,0:T(8,128)}, u32[]{:S(2)}) copy-start(f32[416,108]{1,0:T(8,128)} %copy-done.2) | copy-start | bytes 539140
  87.8 9.5 %collective-permute-start.2 = (f32[182,128]{1,0:T(8,128)S(1)}, f32[182,128]{1,0:T(8,128)S(1)}, u32[]{:S(2)}, u32[]{:S(2)}) collective-permute-start(f32[182,128]{1,0:T(8,128)S(1)} %pad_maximum_fusion.3), channel_id=1, source_target_pairs={{0,1},{1,2},{2,3},{3,4},{4,5},{5,6},{6,7},{7,8},{8,9},{9,10},{10,1... | collective-permute-start | bytes 279560 | tf_op jit(solution)/shard_map/ppermute | solution.py:273
  87.9 9.6 %collective-permute-start.3 = (f32[182,128]{1,0:T(8,128)S(1)}, f32[182,128]{1,0:T(8,128)S(1)}, u32[]{:S(2)}, u32[]{:S(2)}) collective-permute-start(f32[182,128]{1,0:T(8,128)S(1)} %pad_maximum_fusion.4), channel_id=1, source_target_pairs={{1,0},{2,1},{3,2},{4,3},{5,4},{6,5},{7,6},{8,7},{9,8},{10,9},{11,1... | collective-permute-start | bytes 279560 | tf_op jit(solution)/shard_map/ppermute | solution.py:274

commit v7 on v6

--- a/solution.py
+++ b/solution.py
@@ -136,7 +136,7 @@
     copies = []
     for number, peer in enumerate(peers):
         for slot, (source, target) in enumerate(
-            ((blocks_ref.at[peer], held.at[here_col]), (gram_ref, gram_held.at[here_col]))
+            ((blocks_ref.at[peer], held.at[here_col]), (gram_ref.at[peer], gram_held.at[here_col]))
         ):
             copy = pltpu.make_async_remote_copy(
                 src_ref=source,
@@ -149,7 +149,7 @@
             copy.start()
             copies.append(copy)
     held[here_col] = blocks_ref[here_col]
-    gram_held[here_col] = gram_ref[...]
+    gram_held[here_col] = gram_ref[here_col]
     for copy in copies:
         copy.wait()
     sums = held[0]
@@ -158,27 +158,43 @@
         sums = sums + held[source]
         grams = grams + gram_held[source]
     sums_ref[...] = sums
-    grams_ref[...] = grams
+    grams_ref[here_col] = grams
+    copies = []
+    for number, peer in enumerate(peers):
+        copy = pltpu.make_async_remote_copy(
+            src_ref=grams_ref.at[here_col],
+            dst_ref=grams_ref.at[here_col],
+            send_sem=sends.at[2 * cols + number],
+            recv_sem=receipts.at[2 * cols + number],
+            device_id=(here_row, peer),
+            device_id_type=MESH,
+        )
+        copy.start()
+        copies.append(copy)
+    for copy in copies:
+        copy.wait()
 
 
 def col_scatter(blocks, gram):
     cols = blocks.shape[0]
-    return pl.pallas_call(
+    gram_blocks = gram.reshape(cols, -1, gram.shape[1])
+    sums, grams = pl.pallas_call(
         functools.partial(scatter_kernel, cols),
         out_shape=(
             jax.ShapeDtypeStruct(blocks.shape[1:], jnp.float32),
-            jax.ShapeDtypeStruct(gram.shape, jnp.float32),
+            jax.ShapeDtypeStruct(gram_blocks.shape, jnp.float32),
         ),
         in_specs=[pl.BlockSpec(memory_space=pltpu.VMEM)] * 2,
         out_specs=(pl.BlockSpec(memory_space=pltpu.VMEM),) * 2,
         scratch_shapes=[
             pltpu.VMEM(blocks.shape, jnp.float32),
-            pltpu.VMEM((cols,) + gram.shape, jnp.float32),
-            pltpu.SemaphoreType.DMA((2 * cols,)),
-            pltpu.SemaphoreType.DMA((2 * cols,)),
+            pltpu.VMEM(gram_blocks.shape, jnp.float32),
+            pltpu.SemaphoreType.DMA((3 * cols,)),
+            pltpu.SemaphoreType.DMA((3 * cols,)),
         ],
         compiler_params=pltpu.CompilerParams(collective_id=1, has_side_effects=True),
-    )(blocks, gram)
+    )(blocks, gram_blocks)
+    return sums, grams.reshape(gram.shape)
 
 
 def gather_kernel(rows, piece_ref, out_ref, sends, receipts):

time: 193 us -> 181 us (0.938)
  Pallas kernels: 108 us -> 97.8 us
    pallas_call x1, Pallas kernels: 38.9 us -> 28.4 us  [col_scatter(): pl.pallas_call(functools.partial(scatter_kernel, cols), out_shape=(jax.Sh...]
  transfers between devices with their start and end apart: 4 -> 4, of which waited for: 2 -> 2; matrix products, arithmetic and copies ran while one was open for 6% -> 7% of each run, Pallas kernels for 0% -> 0%
where the time goes in v7:
time: 181 us; the launch traced here: 179 us
  Pallas kernels  97.8 us (54%)
  matrix products  24.4 us (13%)
  other arithmetic  20.4 us (11%)
  local copies, waits for them, and re-layouts  13.2 us (7%)
  starting transfers between devices  11.6 us (6%)
  between operations  9.52 us (5%)
  waiting for transfers between devices  2.17 us (1%)
    pallas_call x4, Pallas kernels, grid_totals(): pl.pallas_call(functools.partial(total_kernel, rows, cols), out_shape=jax...  56.1 us
    pallas_call x1, Pallas kernels, col_scatter(): pl.pallas_call(functools.partial(scatter_kernel, cols), out_shape=(jax.Sh...  28.4 us
    pallas_call x1, Pallas kernels, row_gather(): pl.pallas_call(functools.partial(gather_kernel, rows), out_shape=jax.Shap...  13.2 us
    another operation x4, other arithmetic, grid_totals(): lanes = jnp.pad(jnp.stack(parts), (0, 128 - len(parts)))  8.23 us
    dot_general x1, matrix products, body(): jnp.einsum('kij,kjr->ir', hyperspectral, hyper_pairs, preferred_element_t...  7.49 us
    ppermute x1, starting transfers between devices, body(): lax.ppermute(heads, grid, [((i + 1) % count, i) for i in range(count)])  6.57 us
    dot_general x7, matrix products, apply_band(): return jnp.dot(matrix, values.astype(jnp.float32), precision=FULL_PRECISION)  5.99 us
    slice x4, local copies, waits for them, and re-layouts, grid_totals(): return [summed[0, number] for number in range(len(parts))]  5.41 us
  transfers between devices with their start and end apart: 4, of which 2 were waited for; matrix products, arithmetic and copies ran while one was open for 7% of the time, Pallas kernels for 0%

profile of v7, /device:TPU:0, one launch (start us, length us, event | category | flops | bytes accessed | tf_op | source)
XLA Modules:
  0.0 179.0 jit_solution(6050177678492908810)
XLA Ops:
  0.6 1.3 convert_bitcast_fusion.1.piece_ref
  2.0 13.2 %shard_map.95 = f32[16,8,512]{2,1,0:T(8,128)} custom-call(f32[8,512]{1,0:T(8,128)} %convert_bitcast_fusion.1.piece_ref), custom_call_target="tpu_custom_call" | custom-call | tf_op jit(solution)/shard_map/pallas_call | solution.py:228
  16.9 1.5 collective-permute-start
  18.3 2.6 %collective-permute-start.1 = (bf16[8,128]{0,1:T(8,128)(2,1)}, bf16[8,128]{0,1:T(8,128)(2,1)}, u32[]{:S(2)}, u32[]{:S(2)}) collective-permute-start(bf16[8,128]{0,1:T(8,128)(2,1)} %get-tuple-element.35), channel_id=1, source_target_pairs={{1,0},{2,1},{3,2},{4,3},{5,4},{6,5},{7,6},{0,7},{9,8},{10,9},{11,1... | collective-permute-start | bytes 6152 | tf_op jit(solution)/shard_map/ppermute | solution.py:33
  21.0 1.2 fusion.25
  22.2 1.4 select_reduce_fusion.1
  26.7 3.7 %convolution_bitcast_fusion = f32[2048,128]{0,1:T(8,128)S(1)} fusion(bf16[2,2048,512]{2,1,0:T(8,128)(2,1)} %param.8, f32[512,128]{0,1:T(8,128)S(1)} %get-tuple-element.24, f32[2,128]{1,0:T(2,128)S(1)} %fusion.47), kind=kOutput, calls=%fused_computation.4 | convolution fusion | flops 537133056 | bytes 5506048 | tf_op jit(solution)/shard_map/kij,kjr->ir/dot_general | solution.py:255
  31.9 1.5 fusion.14
  33.8 7.5 %fusion.3 = f32[512,128]{0,1:T(8,128)S(1)} fusion(bf16[96,512,128]{2,1,0:T(8,128)(2,1)} %param.9, f32[128,128]{0,1:T(8,128)S(1)} %copy.14, f32[96,128]{1,0:T(8,128)S(1)} %copy-done.2), kind=kOutput, calls=%fused_computation.12 | convolution fusion | flops 1613758464 | bytes 12959744 | tf_op jit(solution)/shard_map/kij,kjr->ir/dot_general | solution.py:258
  43.3 28.4 %shard_map.96 = (f32[320,128]{1,0:T(8,128)}, f32[8,32,128]{2,1,0:T(8,128)}) custom-call(f32[8,320,128]{2,1,0:T(8,128)} %pad_maximum_fusion.blocks_ref, f32[8,32,128]{2,1,0:T(8,128)} %bitcast.88), custom_call_target="tpu_custom_call" | custom-call | tf_op jit(solution)/shard_map/pallas_call | solution.py:181
  77.4 6.6 %collective-permute-start.3 = (f32[182,128]{1,0:T(8,128)S(1)}, f32[182,128]{1,0:T(8,128)S(1)}, u32[]{:S(2)}, u32[]{:S(2)}) collective-permute-start(f32[182,128]{1,0:T(8,128)S(1)} %pad_maximum_fusion.4), channel_id=1, source_target_pairs={{1,0},{2,1},{3,2},{4,3},{5,4},{6,5},{7,6},{8,7},{9,8},{10,9},{11,1... | collective-permute-start | bytes 279560 | tf_op jit(solution)/shard_map/ppermute | solution.py:290
  84.5 1.7 collective-permute-done.3
  90.2 2.1 %select_maximum_fusion.6 = f32[128]{0:T(128)S(1)} fusion(f32[1]{0:T(128)} %bitcast.15, f32[1]{0:T(128)} %bitcast.14, f32[1]{0:T(128)} %bitcast.13), kind=kLoop, calls=%fused_computation.85 | loop fusion | flops 1024 | bytes 524 | tf_op jit(solution)/shard_map/stack | solution.py:110
  92.9 15.9 %shard_map.97 = f32[8,128]{1,0:T(8,128)} custom-call(f32[8,128]{1,0:T(8,128)} %broadcast_in_dim.76.part_ref), custom_call_target="tpu_custom_call" | custom-call | tf_op jit(solution)/shard_map/pallas_call | solution.py:112
  108.7 1.4 fusion.46
  116.3 2.1 %select_maximum_fusion.4 = f32[128]{0:T(128)S(1)} fusion(f32[1]{0:T(128)} %bitcast.22, f32[1]{0:T(128)} %bitcast.21, f32[1]{0:T(128)} %bitcast.20), kind=kLoop, calls=%fused_computation.82 | loop fusion | flops 768 | bytes 524 | tf_op jit(solution)/shard_map/stack | solution.py:110
  119.0 12.9 %shard_map.98 = f32[8,128]{1,0:T(8,128)} custom-call(f32[8,128]{1,0:T(8,128)} %broadcast_in_dim.77.part_ref), custom_call_target="tpu_custom_call" | custom-call | tf_op jit(solution)/shard_map/pallas_call | solution.py:112
  131.9 1.4 fusion.45
  137.5 2.1 %select_maximum_fusion.2 = f32[128]{0:T(128)S(1)} fusion(f32[1]{0:T(128)} %bitcast.28, f32[1]{0:T(128)} %bitcast.27, f32[1]{0:T(128)} %bitcast.26), kind=kLoop, calls=%fused_computation.80 | loop fusion | flops 768 | bytes 524 | tf_op jit(solution)/shard_map/stack | solution.py:110
  140.1 13.8 %shard_map.99 = f32[8,128]{1,0:T(8,128)} custom-call(f32[8,128]{1,0:T(8,128)} %broadcast_in_dim.78.part_ref), custom_call_target="tpu_custom_call" | custom-call | tf_op jit(solution)/shard_map/pallas_call | solution.py:112
  153.9 1.4 fusion.44
  159.5 2.1 %select_maximum_fusion = f32[128]{0:T(128)S(1)} fusion(f32[1]{0:T(128)} %bitcast.34, f32[1]{0:T(128)} %bitcast.33, f32[1]{0:T(128)} %bitcast.32), kind=kLoop, calls=%fused_computation.78 | loop fusion | flops 768 | bytes 524 | tf_op jit(solution)/shard_map/stack | solution.py:110
  162.2 13.6 %shard_map.100 = f32[8,128]{1,0:T(8,128)} custom-call(f32[8,128]{1,0:T(8,128)} %broadcast_in_dim.79.part_ref), custom_call_target="tpu_custom_call" | custom-call | tf_op jit(solution)/shard_map/pallas_call | solution.py:112
  175.8 1.2 slice.196
  (72 shorter events, 29.2 us)
Async XLA Ops:
  0.6 24.1 %copy-start = (f32[2,96]{1,0:T(2,128)S(1)}, f32[2,96]{1,0:T(2,128)}, u32[]{:S(2)}) copy-start(f32[2,96]{1,0:T(2,128)} %param.13) | copy-start | bytes 2308
  16.9 15.0 %collective-permute-start = (bf16[8,128]{0,1:T(8,128)(2,1)}, bf16[8,128]{0,1:T(8,128)(2,1)}, u32[]{:S(2)}, u32[]{:S(2)}) collective-permute-start(bf16[8,128]{0,1:T(8,128)(2,1)} %get-tuple-element.34), channel_id=1, source_target_pairs={{0,1},{1,2},{2,3},{3,4},{4,5},{5,6},{6,7},{7,0},{8,9},{9,10},{10,1... | collective-permute-start | bytes 6152 | tf_op jit(solution)/shard_map/ppermute | solution.py:31
  18.3 13.5 %collective-permute-start.1 = (bf16[8,128]{0,1:T(8,128)(2,1)}, bf16[8,128]{0,1:T(8,128)(2,1)}, u32[]{:S(2)}, u32[]{:S(2)}) collective-permute-start(bf16[8,128]{0,1:T(8,128)(2,1)} %get-tuple-element.35), channel_id=1, source_target_pairs={{1,0},{2,1},{3,2},{4,3},{5,4},{6,5},{7,6},{0,7},{9,8},{10,9},{11,1... | collective-permute-start | bytes 6152 | tf_op jit(solution)/shard_map/ppermute | solution.py:33
  26.6 3.7 %copy-start.3 = (f32[9]{0:T(128)S(1)}, f32[9]{0:T(128)}, u32[]{:S(2)}) copy-start(f32[9]{0:T(128)} %param.14) | copy-start | bytes 112
  26.6 3.7 %copy-start.4 = (s32[9]{0:T(128)S(1)}, s32[9]{0:T(128)}, u32[]{:S(2)}) copy-start(s32[9]{0:T(128)} %param.15) | copy-start | bytes 112
  30.4 3.4 %copy-start.2 = (f32[96,128]{1,0:T(8,128)S(1)}, f32[96,128]{1,0:T(8,128)}, u32[]{:S(2)}) copy-start(f32[96,128]{1,0:T(8,128)} %param.12) | copy-start | bytes 147460
  41.4 32.7 %copy-start.1 = (f32[256,128]{1,0:T(8,128)S(1)}, f32[256,128]{1,0:T(8,128)}, u32[]{:S(2)}) copy-start(f32[256,128]{1,0:T(8,128)} %param.10) | copy-start | bytes 393220
  74.9 9.5 %collective-permute-start.2 = (f32[182,128]{1,0:T(8,128)S(1)}, f32[182,128]{1,0:T(8,128)S(1)}, u32[]{:S(2)}, u32[]{:S(2)}) collective-permute-start(f32[182,128]{1,0:T(8,128)S(1)} %pad_maximum_fusion.3), channel_id=1, source_target_pairs={{0,1},{1,2},{2,3},{3,4},{4,5},{5,6},{6,7},{7,8},{8,9},{9,10},{10,1... | collective-permute-start | bytes 279560 | tf_op jit(solution)/shard_map/ppermute | solution.py:289
  77.4 8.7 %collective-permute-start.3 = (f32[182,128]{1,0:T(8,128)S(1)}, f32[182,128]{1,0:T(8,128)S(1)}, u32[]{:S(2)}, u32[]{:S(2)}) collective-permute-start(f32[182,128]{1,0:T(8,128)S(1)} %pad_maximum_fusion.4), channel_id=1, source_target_pairs={{1,0},{2,1},{3,2},{4,3},{5,4},{6,5},{7,6},{8,7},{9,8},{10,9},{11,1... | collective-permute-start | bytes 279560 | tf_op jit(solution)/shard_map/ppermute | solution.py:290

commit v8 on v7

--- a/solution.py
+++ b/solution.py
@@ -252,9 +252,11 @@
         jnp.bfloat16
     )
     hyper_pairs = (band_factor[:, None, :] * coarse_columns[None, :, :]).astype(jnp.bfloat16)
-    multi_part = jnp.einsum(
-        "kij,kjr->ir", multispectral, multi_pairs, preferred_element_type=jnp.float32
-    )
+    multi_part = jnp.dot(multispectral[0], multi_pairs[0], preferred_element_type=jnp.float32)
+    for band in range(1, multispectral.shape[0]):
+        multi_part = multi_part + jnp.dot(
+            multispectral[band], multi_pairs[band], preferred_element_type=jnp.float32
+        )
     hyper_part = jnp.einsum(
         "kij,kjr->ir", hyperspectral, hyper_pairs, preferred_element_type=jnp.float32
     )

time: 181 us -> 181 us (level)
    dot_general x1 -> x2, matrix products: 3.69 us -> 4.85 us  [the longest x1 2.44 us: body(): jnp.dot(multispectral[band], multi_pairs[band], preferred_element_type=jn...]
where the time goes in v8:
time: 181 us; the launch traced here: 178 us
  Pallas kernels  97.8 us (54%)
  matrix products  25.5 us (14%)
  other arithmetic  19.1 us (11%)
  local copies, waits for them, and re-layouts  12.7 us (7%)
  starting transfers between devices  11.7 us (6%)
  between operations  9.53 us (5%)
  waiting for transfers between devices  2.17 us (1%)
    pallas_call x4, Pallas kernels, grid_totals(): pl.pallas_call(functools.partial(total_kernel, rows, cols), out_shape=jax...  56.1 us
    pallas_call x1, Pallas kernels, col_scatter(): pl.pallas_call(functools.partial(scatter_kernel, cols), out_shape=(jax.Sh...  28.4 us
    pallas_call x1, Pallas kernels, row_gather(): pl.pallas_call(functools.partial(gather_kernel, rows), out_shape=jax.Shap...  13.2 us
    another operation x4, other arithmetic, grid_totals(): lanes = jnp.pad(jnp.stack(parts), (0, 128 - len(parts)))  8.23 us
    dot_general x1, matrix products, body(): jnp.einsum('kij,kjr->ir', hyperspectral, hyper_pairs, preferred_element_t...  7.48 us
    ppermute x1, starting transfers between devices, body(): lax.ppermute(heads, grid, [((i + 1) % count, i) for i in range(count)])  6.57 us
    dot_general x7, matrix products, apply_band(): return jnp.dot(matrix, values.astype(jnp.float32), precision=FULL_PRECISION)  5.96 us
    slice x4, local copies, waits for them, and re-layouts, grid_totals(): return [summed[0, number] for number in range(len(parts))]  5.41 us
  transfers between devices with their start and end apart: 4, of which 2 were waited for; matrix products, arithmetic and copies ran while one was open for 7% of the time, Pallas kernels for 0%

profile of v8, /device:TPU:0, one launch (start us, length us, event | category | flops | bytes accessed | tf_op | source)
XLA Modules:
  0.0 178.4 jit_solution(3909321803154886263)
XLA Ops:
  0.6 1.3 convert_bitcast_fusion.1.piece_ref
  2.0 13.2 %shard_map.95 = f32[16,8,512]{2,1,0:T(8,128)} custom-call(f32[8,512]{1,0:T(8,128)} %convert_bitcast_fusion.1.piece_ref), custom_call_target="tpu_custom_call" | custom-call | tf_op jit(solution)/shard_map/pallas_call | solution.py:228
  16.2 1.5 collective-permute-start
  17.7 2.6 %collective-permute-start.1 = (bf16[8,128]{0,1:T(8,128)(2,1)S(1)}, bf16[8,128]{0,1:T(8,128)(2,1)S(1)}, u32[]{:S(2)}, u32[]{:S(2)}) collective-permute-start(bf16[8,128]{0,1:T(8,128)(2,1)S(1)} %get-tuple-element.33), channel_id=1, source_target_pairs={{1,0},{2,1},{3,2},{4,3},{5,4},{6,5},{7,6},{0,7},{9,8},{10,9},{11,1... | collective-permute-start | bytes 6152 | tf_op jit(solution)/shard_map/ppermute | solution.py:33
  20.5 1.2 fusion.29
  22.7 2.4 %fusion.5 = f32[128,2048]{1,0:T(8,128)S(1)} fusion(bf16[2,2048,512]{2,1,0:T(8,128)(2,1)} %param.8, bf16[2,512,128]{2,1,0:T(8,128)(2,1)S(1)} %multiply_convert_fusion.4), kind=kOutput, calls=%fused_computation.9 | convolution fusion | flops 268435456 | bytes 3276800 | tf_op jit(solution)/shard_map/dot_general | solution.py:255
  25.2 2.4 %fusion.3 = f32[2048,128]{0,1:T(8,128)S(1)} fusion(f32[128,2048]{1,0:T(8,128)S(1)} %fusion.5, bf16[2,2048,512]{2,1,0:T(8,128)(2,1)} %param.8, bf16[2,512,128]{2,1,0:T(8,128)(2,1)S(1)} %multiply_convert_fusion.4), kind=kOutput, calls=%fused_computation.5 | convolution fusion | flops 268697600 | bytes 4325376 | tf_op jit(solution)/shard_map/dot_general | solution.py:257
  31.2 1.5 fusion.18
  33.1 7.5 %fusion.9 = f32[512,128]{0,1:T(8,128)S(1)} fusion(bf16[96,512,128]{2,1,0:T(8,128)(2,1)} %param.9, f32[128,128]{0,1:T(8,128)S(1)} %copy.16, f32[96,128]{1,0:T(8,128)S(1)} %copy-done.2), kind=kOutput, calls=%fused_computation.18 | convolution fusion | flops 1613758464 | bytes 12959744 | tf_op jit(solution)/shard_map/kij,kjr->ir/dot_general | solution.py:260
  42.6 28.4 %shard_map.96 = (f32[320,128]{1,0:T(8,128)}, f32[8,32,128]{2,1,0:T(8,128)}) custom-call(f32[8,320,128]{2,1,0:T(8,128)} %pad_maximum_fusion.blocks_ref, f32[8,32,128]{2,1,0:T(8,128)} %bitcast.96), custom_call_target="tpu_custom_call" | custom-call | tf_op jit(solution)/shard_map/pallas_call | solution.py:181
  76.7 6.6 %collective-permute-start.3 = (f32[182,128]{1,0:T(8,128)S(1)}, f32[182,128]{1,0:T(8,128)S(1)}, u32[]{:S(2)}, u32[]{:S(2)}) collective-permute-start(f32[182,128]{1,0:T(8,128)S(1)} %pad_maximum_fusion.4), channel_id=1, source_target_pairs={{1,0},{2,1},{3,2},{4,3},{5,4},{6,5},{7,6},{8,7},{9,8},{10,9},{11,1... | collective-permute-start | bytes 279560 | tf_op jit(solution)/shard_map/ppermute | solution.py:292
  83.8 1.7 collective-permute-done.3
  89.5 2.1 %select_maximum_fusion.6 = f32[128]{0:T(128)S(1)} fusion(f32[1]{0:T(128)} %bitcast.18, f32[1]{0:T(128)} %bitcast.17, f32[1]{0:T(128)} %bitcast.16), kind=kLoop, calls=%fused_computation.91 | loop fusion | flops 1024 | bytes 524 | tf_op jit(solution)/shard_map/stack | solution.py:110
  92.2 15.8 %shard_map.97 = f32[8,128]{1,0:T(8,128)} custom-call(f32[8,128]{1,0:T(8,128)} %broadcast_in_dim.76.part_ref), custom_call_target="tpu_custom_call" | custom-call | tf_op jit(solution)/shard_map/pallas_call | solution.py:112
  108.0 1.4 fusion.49
  115.6 2.1 %select_maximum_fusion.4 = f32[128]{0:T(128)S(1)} fusion(f32[1]{0:T(128)} %bitcast.25, f32[1]{0:T(128)} %bitcast.24, f32[1]{0:T(128)} %bitcast.23), kind=kLoop, calls=%fused_computation.88 | loop fusion | flops 768 | bytes 524 | tf_op jit(solution)/shard_map/stack | solution.py:110
  118.2 13.0 %shard_map.98 = f32[8,128]{1,0:T(8,128)} custom-call(f32[8,128]{1,0:T(8,128)} %broadcast_in_dim.77.part_ref), custom_call_target="tpu_custom_call" | custom-call | tf_op jit(solution)/shard_map/pallas_call | solution.py:112
  131.2 1.4 fusion.48
  136.8 2.1 %select_maximum_fusion.2 = f32[128]{0:T(128)S(1)} fusion(f32[1]{0:T(128)} %bitcast.31, f32[1]{0:T(128)} %bitcast.30, f32[1]{0:T(128)} %bitcast.29), kind=kLoop, calls=%fused_computation.86 | loop fusion | flops 768 | bytes 524 | tf_op jit(solution)/shard_map/stack | solution.py:110
  139.5 13.7 %shard_map.99 = f32[8,128]{1,0:T(8,128)} custom-call(f32[8,128]{1,0:T(8,128)} %broadcast_in_dim.78.part_ref), custom_call_target="tpu_custom_call" | custom-call | tf_op jit(solution)/shard_map/pallas_call | solution.py:112
  153.2 1.4 fusion.47
  158.8 2.1 %select_maximum_fusion = f32[128]{0:T(128)S(1)} fusion(f32[1]{0:T(128)} %bitcast.37, f32[1]{0:T(128)} %bitcast.36, f32[1]{0:T(128)} %bitcast.35), kind=kLoop, calls=%fused_computation.84 | loop fusion | flops 768 | bytes 524 | tf_op jit(solution)/shard_map/stack | solution.py:110
  161.5 13.6 %shard_map.100 = f32[8,128]{1,0:T(8,128)} custom-call(f32[8,128]{1,0:T(8,128)} %broadcast_in_dim.79.part_ref), custom_call_target="tpu_custom_call" | custom-call | tf_op jit(solution)/shard_map/pallas_call | solution.py:112
  175.1 1.2 slice.212
  (75 shorter events, 28.7 us)
Async XLA Ops:
  0.6 21.1 %copy-start = (f32[2,96]{1,0:T(2,128)S(1)}, f32[2,96]{1,0:T(2,128)}, u32[]{:S(2)}) copy-start(f32[2,96]{1,0:T(2,128)} %param.13) | copy-start | bytes 2308
  16.2 15.0 %collective-permute-start = (bf16[8,128]{0,1:T(8,128)(2,1)S(1)}, bf16[8,128]{0,1:T(8,128)(2,1)S(1)}, u32[]{:S(2)}, u32[]{:S(2)}) collective-permute-start(bf16[8,128]{0,1:T(8,128)(2,1)S(1)} %get-tuple-element.32), channel_id=1, source_target_pairs={{0,1},{1,2},{2,3},{3,4},{4,5},{5,6},{6,7},{7,0},{8,9},{9,10},{10,1... | collective-permute-start | bytes 6152 | tf_op jit(solution)/shard_map/ppermute | solution.py:31
  17.7 13.5 %collective-permute-start.1 = (bf16[8,128]{0,1:T(8,128)(2,1)S(1)}, bf16[8,128]{0,1:T(8,128)(2,1)S(1)}, u32[]{:S(2)}, u32[]{:S(2)}) collective-permute-start(bf16[8,128]{0,1:T(8,128)(2,1)S(1)} %get-tuple-element.33), channel_id=1, source_target_pairs={{1,0},{2,1},{3,2},{4,3},{5,4},{6,5},{7,6},{0,7},{9,8},{10,9},{11,1... | collective-permute-start | bytes 6152 | tf_op jit(solution)/shard_map/ppermute | solution.py:33
  25.2 2.5 %copy-start.3 = (f32[9]{0:T(128)S(1)}, f32[9]{0:T(128)}, u32[]{:S(2)}) copy-start(f32[9]{0:T(128)} %param.14) | copy-start | bytes 112
  25.2 2.5 %copy-start.4 = (s32[9]{0:T(128)S(1)}, s32[9]{0:T(128)}, u32[]{:S(2)}) copy-start(s32[9]{0:T(128)} %param.15) | copy-start | bytes 112
  28.8 4.3 %copy-start.2 = (f32[96,128]{1,0:T(8,128)S(1)}, f32[96,128]{1,0:T(8,128)}, u32[]{:S(2)}) copy-start(f32[96,128]{1,0:T(8,128)} %param.12) | copy-start | bytes 147460
  40.7 32.7 %copy-start.1 = (f32[256,128]{1,0:T(8,128)S(1)}, f32[256,128]{1,0:T(8,128)}, u32[]{:S(2)}) copy-start(f32[256,128]{1,0:T(8,128)} %param.10) | copy-start | bytes 393220
  74.3 9.5 %collective-permute-start.2 = (f32[182,128]{1,0:T(8,128)S(1)}, f32[182,128]{1,0:T(8,128)S(1)}, u32[]{:S(2)}, u32[]{:S(2)}) collective-permute-start(f32[182,128]{1,0:T(8,128)S(1)} %pad_maximum_fusion.3), channel_id=1, source_target_pairs={{0,1},{1,2},{2,3},{3,4},{4,5},{5,6},{6,7},{7,8},{8,9},{9,10},{10,1... | collective-permute-start | bytes 279560 | tf_op jit(solution)/shard_map/ppermute | solution.py:291
  76.7 8.7 %collective-permute-start.3 = (f32[182,128]{1,0:T(8,128)S(1)}, f32[182,128]{1,0:T(8,128)S(1)}, u32[]{:S(2)}, u32[]{:S(2)}) collective-permute-start(f32[182,128]{1,0:T(8,128)S(1)} %pad_maximum_fusion.4), channel_id=1, source_target_pairs={{1,0},{2,1},{3,2},{4,3},{5,4},{6,5},{7,6},{8,7},{9,8},{10,9},{11,1... | collective-permute-start | bytes 279560 | tf_op jit(solution)/shard_map/ppermute | solution.py:292
